TPU v7x, 32 devices: a whole 2x2x4 slice. The times are simulated.
32 devices in a mesh: parts: 2 (over x), tile: 16 (over z, y, core).
Axes of the slice: x: 2, y: 2, z: 4, core: 2. Of those that a mesh axis runs over, the one named last changes fastest.
Arguments:
- sections: bfloat16 [4096, 2048], P(('parts', 'tile')), parts along dimension 0, may hold values from -10 to 10
- valid_mask: int32 [32, 16], P(('parts', 'tile')), parts along dimension 0, may hold values 0 or 1
- coarse_offsets: int32 [8, 2], P('parts'), parts along dimension 0, may hold values from -3 to 3
Outputs:
- aligned: bfloat16 [4096, 2048], P(('parts', 'tile')), parts along dimension 0
- node_shift: float32 [2, 32, 16], P(None, ('parts', 'tile')), parts along dimension 1
There are 2 independent parts, one for each index of `parts`. A program takes and returns all parts, laid end to end along the dimension named above; each array names one. Nothing has to cross between parts.
All inputs are finite; a program needn't handle non-finite values. No bound on the sum of `valid_mask` on one device may be relied on, other than what follows from the above.
Results may differ from a plain program's by a relative error of at most 0.002.
Values may be sent and summed in bfloat16 or wider, within the bound.
A program may use at most 64 MiB of HBM per device.

v0:
```python
import functools

import jax
import jax.numpy as jnp
import numpy as np
from jax import lax
from jax.experimental import pallas as pl
from jax.experimental.pallas import tpu as pltpu
from jax.sharding import PartitionSpec as P

SECTIONS = 4
PATCH = 128
HALF = 4
SWEEPS = 3
REACH = 3
WINDOW = 2 * HALF + 1
PADDED = 16
LANES = 128
CONSTANTS = 6
HALVES = 2
PIECES = 2

sharpness = 12.0
anchor_weight = 2.0
MESH = pl.DeviceIdType.MESH
f32 = jnp.float32
bf16 = jnp.bfloat16


def split(value):
    high = value.astype(bf16)
    return high, (value - high.astype(f32)).astype(bf16)


def mm(a, b):
    return jnp.dot(a, b, preferred_element_type=f32)


def mm_nt(a, b):
    return lax.dot_general(a, b, (((1,), (1,)), ((), ())), preferred_element_type=f32)


def mm3(a, b, product=mm):
    return product(a[0], b[0]) + (product(a[0], b[1]) + product(a[1], b[0]))


def constants():
    n = PATCH
    k = np.arange(n)
    angle = 2 * np.pi * ((k[:, None] * k[None, :]) % n) / n
    stacked = np.concatenate([np.cos(angle), np.sin(angle)], axis=0)
    dft_hi = np.asarray(stacked, bf16)
    dft_t_hi = np.asarray(stacked.T, bf16)
    dft_lo = np.asarray(stacked - dft_hi.astype(np.float64), bf16)
    dft_hi2 = np.concatenate([dft_hi, dft_lo], axis=0)
    dft_t_hi2 = np.concatenate([dft_t_hi, np.asarray(stacked.T - dft_t_hi.astype(np.float64), bf16)], axis=1)
    u = np.arange(-HALF - REACH, -HALF - REACH + 24)
    window_angle = 2 * np.pi * ((u[:, None] * k[None, :]) % n) / n
    exact = np.cos(angle)
    gain = (dft_hi[:n].astype(np.float64) * exact).sum(axis=1) / (exact * exact).sum(axis=1)
    window = np.stack([np.cos(window_angle), np.sin(window_angle)])
    window = window.astype(np.float32)
    half_angle = np.pi * k / n
    sign = 1.0 - 2.0 * (k % 2)
    warp = np.zeros((8, n), np.float32)
    warp[:4] = np.stack([np.sin(half_angle), np.cos(half_angle), sign, k])
    parity = (sign[:, None] * sign[None, :]).astype(np.float32)
    sums = (dft_hi.astype(np.float64)+dft_lo.astype(np.float64)).sum(axis=1, keepdims=True)
    sums = np.broadcast_to(sums, (2 * n, n)).astype(np.float32)
    return dft_hi2, dft_t_hi2, sums, window, warp, parity


def shift_terms(d):
    whole = jnp.round(d)
    frac = d - whole
    odd = jnp.abs(whole - 2.0 * jnp.round(whole * 0.5))
    sine = jnp.sin(jnp.pi * frac)
    signed = jnp.where(odd > 0.5, -sine, sine) * (1.0 / PATCH)
    angle = d * (np.pi / PATCH)
    tangent = jnp.sin(angle) / jnp.cos(angle)
    small = frac * (np.pi / PATCH)
    tiny = jnp.abs(frac) < 1e-6
    peak = jnp.where(
        tiny, 1.0, sine * jnp.cos(small) / jnp.where(tiny, 1.0, PATCH * jnp.sin(small))
    )
    return tangent, signed, peak, whole


def kernel_rows(terms, tables):
    columns = jnp.transpose(terms)[:LANES]
    sine, cosine, parity, gap = [tables[i : i + 1, :] for i in range(4)]
    found = []
    for base, forward in ((0, False), (4, True)):
        tangent, signed, peak, whole = [columns[:, base + i : base + i + 1] for i in range(4)]
        if forward:
            bottom = cosine * tangent + sine
            top = cosine - sine * tangent
            centre = jnp.where(whole > 0, PATCH - whole, -whole)
        else:
            bottom = cosine * tangent - sine
            top = cosine + sine * tangent
            centre = jnp.where(whole < 0, whole + PATCH, whole)
        found.append(jnp.where(gap == centre, peak, (signed * parity) * (top / bottom)))
    corner = columns[:, 1:2] * columns[:, 5:6]
    return found[0], found[1], corner


def circulant(row):
    spread = jnp.broadcast_to(row, (PATCH, PATCH))
    return split(pltpu.roll(spread, 0, 1, stride=1, stride_axis=0))


def warp_patch(patch, rows, i, checker, parity):
    left = circulant(rows[0][i : i + 1, :])
    right = circulant(rows[1][i : i + 1, :])
    both = mm(patch, jnp.concatenate(right, axis=1))
    high, low = split(both[:, :PATCH] + both[:, PATCH:])
    lower = jnp.concatenate([high, jnp.zeros_like(low)], axis=1)
    inner = jnp.concatenate([jnp.concatenate([high, low], axis=1), lower], axis=0)
    moved = mm(jnp.concatenate(left, axis=1), inner)
    corner = (rows[2][i : i + 1, :] * checker) * parity
    return (moved[:, :PATCH] + moved[:, PATCH:]) - corner


def total(value):
    return jnp.sum(jnp.sum(value, axis=0, keepdims=True), axis=1, keepdims=True)


def term_rows(d_rows, d_cols):
    both = jnp.concatenate([d_rows, d_cols], axis=0)
    tangent, signed, peak, whole = shift_terms(both)
    pieces = [t[i : i + 1] for i in range(2) for t in (tangent, signed, peak, whole)]
    return jnp.concatenate(pieces, axis=0)


def centred(patch):
    mean_level = total(patch) * (1.0 / (PATCH * PATCH))
    centre = patch - mean_level
    variance = total(centre * centre) * (1.0 / (PATCH * PATCH))
    return mean_level, jnp.sqrt(variance + 1e-05)


def patch_slices(width):
    return [slice(i * PATCH, (i + 1) * PATCH) for i in range(width // PATCH)]


def chain_kernel(
    tile_count,
    grid_cols,
    offsets_in,
    mask_in,
    *rest,
):
    constant_in = rest[:CONSTANTS]
    constant_ref = rest[CONSTANTS + 2 : 2 * CONSTANTS + 2]
    dft_ref, dft_t_ref, sums_ref, window, warp_tables, parity_ref = constant_ref
    strip, out_ref = rest[CONSTANTS : CONSTANTS + 2]
    (
    offsets,
    mask_ref,
    load_sem,
    raw,
    mask_tile,
    mask_slots,
    flow_tile,
    flow_slots,
    flow_sum,
    spec_re,
    spec_im,
    strip_send,
    strip_recv,
    mask_send,
    mask_recv,
    flow_send,
    flow_recv,
    ) = rest[2 * CONSTANTS + 2 :]
    per_section = tile_count // SECTIONS
    me = lax.axis_index("tile")
    lead = per_section // 2
    rotated = lax.rem(me + tile_count - lead, tile_count)
    group = rotated // per_section
    row = lax.rem(rotated, per_section)
    chain = me // per_section
    quarter = raw.shape[3] * HALVES
    part = raw.shape[3]
    quarter_nodes = quarter // PATCH
    part_nodes = part // PATCH
    reach = -(-SWEEPS // quarter_nodes)

    barrier = pltpu.get_barrier_semaphore()
    for step in range(1, tile_count):
        peer = lax.rem(me + step, tile_count)
        pl.semaphore_signal(barrier, inc=1, device_id={"tile": peer}, device_id_type=MESH)

    loads = [
        pltpu.make_async_copy(source, target, load_sem.at[i])
        for i, (source, target) in enumerate(
            zip((mask_in, offsets_in) + constant_in, (mask_ref, offsets) + constant_ref)
        )
    ]
    for copy in loads:
        copy.start()
    def columns(owner, half):
        return strip.at[:, pl.ds(pl.multiple_of(owner * quarter + half * part, LANES), part)]

    for half in range(HALVES):
        pltpu.make_async_copy(
            columns(chain, half), raw.at[group, half], strip_recv.at[group, half]
        ).start()
    loads[0].wait()
    shape = (2 * per_section, LANES)
    sub = lax.broadcasted_iota(jnp.int32, shape, 0)
    lane = lax.broadcasted_iota(jnp.int32, shape, 1)
    sub_row = lax.rem(sub, per_section)
    mask_tile[...] = jnp.zeros(shape, f32)
    mask_tile[0:1, 0:grid_cols] = mask_ref[...].astype(f32)
    mask_row = mask_tile[0:1, :]
    mask_tile[...] = jnp.where(sub_row == row, mask_row, 0.0)
    mask_slots[me] = mask_tile[...]

    pl.semaphore_wait(barrier, tile_count - 1)

    mask_copies = []
    for step in range(1, tile_count):
        peer = lax.rem(me + step, tile_count)
        copy = pltpu.make_async_remote_copy(
            src_ref=mask_tile,
            dst_ref=mask_slots.at[me],
            send_sem=mask_send.at[step],
            recv_sem=mask_recv.at[step],
            device_id={"tile": peer},
            device_id_type=MESH,
        )
        copy.start()
        mask_copies.append(copy)

    sends = []
    for half in range(HALVES):
        for step in range(1, SECTIONS):
            copy = pltpu.make_async_remote_copy(
                src_ref=columns(lax.rem(chain + step, SECTIONS), half),
                dst_ref=raw.at[group, half],
                send_sem=strip_send.at[step, half],
                recv_sem=strip_recv.at[group, half],
                device_id={"tile": lax.rem(me + step * per_section, tile_count)},
                device_id_type=MESH,
            )
            copy.start()
            sends.append(copy)
    for copy in loads[1:]:
        copy.wait()
    tables = warp_tables[...]
    parity = parity_ref[...]
    dft = dft_ref[...]
    dft_t = dft_t_ref[...]
    sums = sums_ref[...]

    def spectra(patches, levels):
        found = []
        for patch, level in zip(patches, levels):
            first = mm(dft, patch)
            first = (first[: 2 * PATCH] + first[2 * PATCH :] - sums * level).astype(bf16)
            both = mm(first, dft_t)
            both = both[:, : 2 * PATCH] + both[:, 2 * PATCH :]
            real = both[:PATCH, :PATCH] - both[PATCH:, PATCH:]
            imag = -(both[:PATCH, PATCH:] + both[PATCH:, :PATCH])
            found.append((real, imag))
        return found

    def patch_of(section, i):
        start = (i % part_nodes) * PATCH
        return raw[section, i // part_nodes, :, start : start + PATCH]

    def own_spectra(section, nodes):
        patches = [patch_of(section, i) for i in nodes]
        pieces = [centred(patch.astype(f32)) for patch in patches]
        found = spectra(patches, [piece[0] for piece in pieces])
        for i, (real, imag) in zip(nodes, found):
            spec_re[i] = real
            spec_im[i] = imag
        return [piece[1] for piece in pieces]

    def checkers(section):
        return [total(patch_of(section, i).astype(f32) * parity) for i in range(quarter_nodes)]

    up_ok = (sub_row > 0).astype(f32)
    down_ok = (sub_row < per_section - 1).astype(f32)
    left_ok = jnp.logical_and(lane > 0, lane < grid_cols).astype(f32)
    right_ok = (lane < grid_cols - 1).astype(f32)
    count = up_ok + down_ok + left_ok + right_ok

    def relax(flow, mask):
        weight = anchor_weight * mask
        pull = weight * flow
        scale = 1.0 / (weight + count)
        d = flow * mask
        for _ in range(SWEEPS):
            near = (
                up_ok * pltpu.roll(d, 1, 0)
                + down_ok * pltpu.roll(d, 2 * per_section - 1, 0)
                + left_ok * pltpu.roll(d, 1, 1)
                + right_ok * pltpu.roll(d, LANES - 1, 1)
            )
            d = (pull + near) * scale
        return jnp.where(lane < grid_cols, d, 0.0)

    corr_row = lax.broadcasted_iota(jnp.int32, (PADDED, PADDED), 0)
    corr_col = lax.broadcasted_iota(jnp.int32, (PADDED, PADDED), 1)
    inside = jnp.logical_and(corr_row < WINDOW, corr_col < WINDOW)

    def arrived(section, half):
        pltpu.make_async_copy(
            raw.at[section, half], raw.at[section, half], strip_recv.at[section, half]
        ).wait()

    def flows(section, previous, own_spread, nodes):
        pieces = [centred(patch.astype(f32)) for patch in previous]
        found = spectra(previous, [piece[0] for piece in pieces])
        row_offset = offsets[0, section]
        col_offset = offsets[1, section]
        row_cos = window[0, pl.ds(row_offset + REACH, PADDED), :]
        row_sin = window[1, pl.ds(row_offset + REACH, PADDED), :]
        col_cos = split(window[0, pl.ds(col_offset + REACH, PADDED), :])
        col_sin = split(window[1, pl.ds(col_offset + REACH, PADDED), :])
        row_table = jnp.concatenate(split(jnp.concatenate([row_cos, row_sin], axis=0)), axis=0)
        row_shift = (corr_row - HALF + row_offset).astype(f32)
        col_shift = (corr_col - HALF + col_offset).astype(f32)
        half_re, half_im = [], []
        for i, (prev_re, prev_im) in zip(nodes, found):
            own_re, own_im = spec_re[i], spec_im[i]
            cross_re = own_re * prev_re + own_im * prev_im
            cross_im = own_im * prev_re - own_re * prev_im
            cross = jnp.concatenate([cross_re, cross_im], axis=1).astype(bf16)
            parts = mm(row_table, cross)
            parts = parts[: 2 * PADDED] + parts[2 * PADDED :]
            part_re = parts[:, :PATCH]
            part_im = parts[:, PATCH:]
            half_re.append(part_re[:PADDED] - part_im[PADDED:])
            half_im.append(part_im[:PADDED] + part_re[PADDED:])
        correlation = mm3(
            split(jnp.concatenate(half_re, axis=0)), col_cos, mm_nt
        ) - mm3(split(jnp.concatenate(half_im, axis=0)), col_sin, mm_nt)
        tile = jnp.zeros(shape, f32)
        for k, i in enumerate(nodes):
            scale = sharpness / (float(PATCH) ** 4 * own_spread[k] * pieces[k][1])
            score = correlation[k * PADDED : (k + 1) * PADDED] * scale
            weights = jnp.where(inside, jnp.exp(score), 0.0)
            inverse = 1.0 / total(weights)
            flow_row = total(weights * row_shift) * inverse
            flow_col = total(weights * col_shift) * inverse
            here = lane == chain * quarter_nodes + i
            tile = jnp.where(jnp.logical_and(here, sub == row), flow_row, tile)
            tile = jnp.where(
                jnp.logical_and(here, sub == row + per_section), flow_col, tile
            )
        return tile

    def receive(index, away):
        def take(other):
            pltpu.make_async_copy(
                flow_slots.at[index, other], flow_slots.at[index, other], flow_recv.at[index, other]
            ).wait()
            return flow_slots[index, other]

        base = (chain + away) * per_section
        if away == 0:
            mine = lax.rem(me, per_section)
            found = flow_sum[index]
            for j in range(1, per_section):
                found = found + take(base + lax.rem(mine + j, per_section))
            flow_sum[index] = found
        else:

            @pl.when(jnp.logical_and(chain + away >= 0, chain + away < SECTIONS))
            def _():
                found = flow_sum[index]
                for j in range(per_section):
                    found = found + take(base + j)
                flow_sum[index] = found

    everyone = list(range(quarter_nodes))
    d = None
    for section in range(1, SECTIONS):
        index = section - 1
        if section == 1:
            tile = jnp.zeros(shape, f32)
            for half in range(HALVES):
                nodes = everyone[half * part_nodes : (half + 1) * part_nodes]
                arrived(1, half)
                arrived(0, half)
                spread = own_spectra(1, nodes)
                previous = [patch_of(0, i) for i in nodes]
                tile = tile + flows(1, previous, spread, nodes)
        else:
            pick_rows = jnp.sum(
                jnp.where(sub == row, d, 0.0), axis=0, keepdims=True
            )
            pick_cols = jnp.sum(
                jnp.where(sub == row + per_section, d, 0.0), axis=0, keepdims=True
            )
            terms = term_rows(pick_rows, pick_cols)
            term_lane = lax.broadcasted_iota(jnp.int32, terms.shape, 1)
            placed = jnp.zeros(terms.shape, f32)
            for i in everyone:
                wanted = term_lane == chain * quarter_nodes + i
                column = jnp.sum(jnp.where(wanted, terms, 0.0), axis=1, keepdims=True)
                placed = jnp.where(term_lane == i, column, placed)
            rows = kernel_rows(placed, tables)
            previous = [
                warp_patch(patch_of(index, i), rows, i, corners[i], parity).astype(bf16)
                for i in everyone
            ]
            tile = flows(section, previous, spread, everyone)
        flow_tile[index] = tile
        flow_sum[index] = tile
        copies = []
        for step in range(1, tile_count):
            peer = lax.rem(me + step, tile_count)
            copy = pltpu.make_async_remote_copy(
                src_ref=flow_tile.at[index],
                dst_ref=flow_slots.at[index, me],
                send_sem=flow_send.at[index, step],
                recv_sem=flow_recv.at[index, me],
                device_id={"tile": peer},
                device_id_type=MESH,
            )
            copy.start()
            copies.append(copy)
        if section == 1:
            for copy in mask_copies:
                copy.wait()
        if section < SECTIONS - 1:
            for half in range(HALVES):
                arrived(section + 1, half)
            spread = own_spectra(section + 1, everyone)
            corners = checkers(section)
            mask = jnp.zeros(shape, f32)
            for r in range(per_section):
                mask = mask + mask_slots[(section * per_section + r + lead) % tile_count]
            for away in range(-reach, reach + 1):
                receive(index, away)
            d = relax(flow_sum[index], mask)
        sends += copies
    mask = jnp.zeros(shape, f32)
    for r in range(per_section):
        mask = mask + mask_slots[
            lax.rem(group * per_section + r + lead, tile_count)
        ]
    for copy in sends:
        copy.wait_send()
    for index in range(SECTIONS - 1):
        for away in range(1 - SECTIONS, SECTIONS):
            if abs(away) > reach or index == SECTIONS - 2:
                receive(index, away)
    flow = jnp.zeros(shape, f32)
    for index in range(SECTIONS - 1):
        flow = jnp.where(group == index + 1, flow_sum[index], flow)
    home = jnp.where(group == 0, 0.0, relax(flow, mask))
    out_row = jnp.sum(jnp.where(sub == row, home, 0.0), axis=0, keepdims=True)
    out_col = jnp.sum(jnp.where(sub == row + per_section, home, 0.0), axis=0, keepdims=True)
    out_ref[...] = jnp.concatenate([out_row, out_col], axis=0)


def warp_kernel(
    shift_ref, strip_in, warp_tables, parity_ref, out, node_ref, strip, result, sems
):
    pieces = strip.shape[0]
    width = strip.shape[2]
    loads, stores = [], []
    for k in range(pieces):
        where = pl.ds(k * width, width)
        loads.append(pltpu.make_async_copy(strip_in.at[:, where], strip.at[k], sems.at[k]))
        stores.append(
            pltpu.make_async_copy(result.at[k], out.at[:, where], sems.at[pieces + k])
        )
        loads[k].start()
    nodes = node_ref.shape[2]
    node_ref[0] = shift_ref[0:1, 0:nodes]
    node_ref[1] = shift_ref[1:2, 0:nodes]
    rows = kernel_rows(term_rows(shift_ref[0:1, :], shift_ref[1:2, :]), warp_tables[...])
    parity = parity_ref[...]
    for k in range(pieces):
        loads[k].wait()
        for j, s in enumerate(patch_slices(width)):
            i = k * (width // PATCH) + j
            patch = strip[k, :, s]
            checker = total(patch.astype(f32) * parity)
            result[k, :, s] = warp_patch(patch, rows, i, checker, parity).astype(bf16)
        stores[k].start()
    for copy in stores:
        copy.wait()


def shards(tile_count, sections, valid_mask, coarse_offsets):
    per_section = tile_count // SECTIONS
    grid_cols = valid_mask.shape[1]
    quarter = sections.shape[1] // SECTIONS
    nodes = quarter // PATCH
    steps = SECTIONS - 1
    tile_shape = (2 * per_section, LANES)
    vmem = pl.BlockSpec(memory_space=pltpu.VMEM)
    tables = constants()
    hbm = pl.BlockSpec(memory_space=pltpu.HBM)
    shift = pl.pallas_call(
        functools.partial(chain_kernel, tile_count, grid_cols),
        out_shape=jax.ShapeDtypeStruct((2, LANES), f32),
        in_specs=[hbm] * (CONSTANTS + 3),
        out_specs=vmem,
        scratch_shapes=[pltpu.VMEM(table.shape, table.dtype) for table in tables]
        + [
            pltpu.SMEM(coarse_offsets.shape[::-1], jnp.int32),
            pltpu.VMEM(valid_mask.shape, jnp.int32),
            pltpu.SemaphoreType.DMA((CONSTANTS + 2,)),
            pltpu.VMEM((SECTIONS, HALVES, PATCH, quarter // HALVES), bf16),
            pltpu.VMEM(tile_shape, f32),
            pltpu.VMEM((tile_count,) + tile_shape, f32),
            pltpu.VMEM((steps,) + tile_shape, f32),
            pltpu.VMEM((steps, tile_count) + tile_shape, f32),
            pltpu.VMEM((steps,) + tile_shape, f32),
            pltpu.VMEM((nodes, PATCH, PATCH), f32),
            pltpu.VMEM((nodes, PATCH, PATCH), f32),
            pltpu.SemaphoreType.DMA((SECTIONS, HALVES)),
            pltpu.SemaphoreType.DMA((SECTIONS, HALVES)),
            pltpu.SemaphoreType.DMA((tile_count,)),
            pltpu.SemaphoreType.DMA((tile_count,)),
            pltpu.SemaphoreType.DMA((steps, tile_count)),
            pltpu.SemaphoreType.DMA((steps, tile_count)),
        ],
        compiler_params=pltpu.CompilerParams(
            collective_id=0, has_side_effects=True
        ),
        name="chain",
    )(coarse_offsets.T, valid_mask, *tables, sections)
    return pl.pallas_call(
        warp_kernel,
        out_shape=(
            jax.ShapeDtypeStruct(sections.shape, bf16),
            jax.ShapeDtypeStruct((2, 1, grid_cols), f32),
        ),
        in_specs=[vmem, hbm, vmem, vmem],
        out_specs=(hbm, vmem),
        scratch_shapes=[
            pltpu.VMEM((PIECES, PATCH, sections.shape[1] // PIECES), bf16),
            pltpu.VMEM((PIECES, PATCH, sections.shape[1] // PIECES), bf16),
            pltpu.SemaphoreType.DMA((2 * PIECES,)),
        ],
        name="warp",
    )(shift, sections, tables[-2], tables[-1])


def solution(mesh):
    placed = (P(("parts", "tile"), None), P(("parts", "tile"), None), P("parts", None))
    return jax.shard_map(
        functools.partial(shards, mesh.shape["tile"]),
        mesh=mesh,
        in_specs=placed,
        out_specs=(P(("parts", "tile"), None), P(None, ("parts", "tile"), None)),
        check_vma=False,
    )
```

profile of v0, /device:TPU:0, one launch (start us, length us, event | category | flops | bytes accessed | tf_op | source)
XLA Modules:
  0.0 45.0 jit_solution(9505668731884425519)
XLA Ops:
  0.6 39.9 %chain.1.shift_ref = f32[2,128]{1,0:T(2,128)} custom-call(s32[2,4]{1,0:T(2,128)} %bitcast.1, s32[1,16]{1,0:T(1,128)} %mask_in.1, bf16[512,128]{1,0:T(8,128)(2,1)} %constant.12.clone.rest_0_, bf16[128,512]{1,0:T(8,128)(2,1)} %constant.13.clone.rest_1_, f32[256,128]{1,0:T(8,128)} %constant.14.clone.rest_2_, f32[2,24,128]{2,1,0:T(8,128)} %constant.15.clone.rest_3_, ...), custom_call_target="tpu_custom_call" | custom-call | tf_op jit(solution)/shard_map/chain/pallas_call | solution.py:504
  40.5 4.5 %warp.1 = (bf16[128,2048]{1,0:T(8,128)(2,1)}, f32[2,1,16]{2,1,0:T(1,128)}) custom-call(f32[2,128]{1,0:T(2,128)} %chain.1.shift_ref, bf16[128,2048]{1,0:T(8,128)(2,1)} %strip_in.1, f32[8,128]{1,0:T(8,128)} %constant.16.clone.rest_4_.warp_tables, f32[128,128]{1,0:T(8,128)} %constant.17.clone.rest_5_.parity_ref), custom_call_target="tpu_custom_call" | custom-call | tf_op jit(solution)/shard_map/warp/pallas_call | solution.py:534
where the time goes:
time: 45.2 us; the launch traced here: 45 us
  Pallas kernels  44.3 us (98%)
  between operations  0.64 us (1%)
    pallas_call x1, Pallas kernels, shards(): pl.pallas_call(functools.partial(chain_kernel, tile_count, grid_cols), ou...  39.9 us
    pallas_call x1, Pallas kernels, shards(): pl.pallas_call(warp_kernel, out_shape=(jax.ShapeDtypeStruct(sections.shap...  4.49 us

commit v1 on v0

v1 whole, which is shorter than its diff:
```python
import functools

import jax
import jax.numpy as jnp
import numpy as np
from jax import lax
from jax.experimental import pallas as pl
from jax.experimental.pallas import tpu as pltpu
from jax.sharding import PartitionSpec as P

SECTIONS = 4
PATCH = 128
HALF = 4
SWEEPS = 3
REACH = 3
WINDOW = 2 * HALF + 1
PADDED = 16
LANES = 128
CHUNK = 2
PIECES = 2

sharpness = 12.0
anchor_weight = 2.0
MESH = pl.DeviceIdType.MESH
f32 = jnp.float32
bf16 = jnp.bfloat16


def split(value):
    high = value.astype(bf16)
    return high, (value - high.astype(f32)).astype(bf16)


def mm(a, b):
    return jnp.dot(a, b, preferred_element_type=f32)


def mm_nt(a, b):
    return lax.dot_general(a, b, (((1,), (1,)), ((), ())), preferred_element_type=f32)


def constants():
    n = PATCH
    k = np.arange(n)
    angle = 2 * np.pi * ((k[:, None] * k[None, :]) % n) / n
    cosine, sine = np.cos(angle), np.sin(angle)
    left = []
    for table in (cosine, sine):
        high = np.asarray(table, bf16)
        low = np.asarray(table - high.astype(np.float64), bf16)
        left.append(np.concatenate([high, low], axis=1))
    left = np.concatenate(left, axis=0)
    right = np.block([[cosine, -sine], [-sine, -cosine]])
    right = np.asarray(right, bf16)
    u = np.arange(-HALF - REACH, -HALF - REACH + 24)
    window_angle = 2 * np.pi * ((u[:, None] * k[None, :]) % n) / n
    window = np.stack([np.cos(window_angle), np.sin(window_angle)])
    window = window.astype(np.float32)
    half_angle = np.pi * k / n
    sign = 1.0 - 2.0 * (k % 2)
    warp = np.zeros((8, n), np.float32)
    warp[:4] = np.stack([np.sin(half_angle), np.cos(half_angle), sign, k])
    parity = (sign[:, None] * sign[None, :]).astype(np.float32)
    return left, right, window, warp, parity


def turn(value):
    small = (value - jnp.round(value)) * np.pi
    square = small * small
    sine = small * (1.0 + square * (-1 / 6 + square * (1 / 120 + square * (
        -1 / 5040 + square * (1 / 362880 - square * (1 / 39916800))))))
    cosine = 1.0 + square * (-1 / 2 + square * (1 / 24 + square * (-1 / 720 + square * (
        1 / 40320 + square * (-1 / 3628800 + square * (1 / 479001600))))))
    return 1.0 - 2.0 * (sine * sine), 2.0 * (sine * cosine)


def shift_terms(d):
    whole = jnp.round(d)
    frac = d - whole
    odd = jnp.abs(whole - 2.0 * jnp.round(whole * 0.5))
    sine = jnp.sin(jnp.pi * frac)
    signed = jnp.where(odd > 0.5, -sine, sine) * (1.0 / PATCH)
    angle = d * (np.pi / PATCH)
    tangent = jnp.sin(angle) / jnp.cos(angle)
    small = frac * (np.pi / PATCH)
    tiny = jnp.abs(frac) < 1e-6
    peak = jnp.where(
        tiny, 1.0, sine * jnp.cos(small) / jnp.where(tiny, 1.0, PATCH * jnp.sin(small))
    )
    return tangent, signed, peak, whole


def kernel_rows(terms, tables):
    columns = jnp.transpose(terms)[:LANES]
    sine, cosine, parity, gap = [tables[i : i + 1, :] for i in range(4)]
    found = []
    for base, forward in ((0, False), (4, True)):
        tangent, signed, peak, whole = [columns[:, base + i : base + i + 1] for i in range(4)]
        if forward:
            bottom = cosine * tangent + sine
            top = cosine - sine * tangent
            centre = jnp.where(whole > 0, PATCH - whole, -whole)
        else:
            bottom = cosine * tangent - sine
            top = cosine + sine * tangent
            centre = jnp.where(whole < 0, whole + PATCH, whole)
        found.append(jnp.where(gap == centre, peak, (signed * parity) * (top / bottom)))
    corner = columns[:, 1:2] * columns[:, 5:6]
    return found[0], found[1], corner


def circulant(row):
    spread = jnp.broadcast_to(row, (PATCH, PATCH))
    return split(pltpu.roll(spread, 0, 1, stride=1, stride_axis=0))


def warp_patch(patch, rows, i, checker, parity):
    left = circulant(rows[0][i : i + 1, :])
    right = circulant(rows[1][i : i + 1, :])
    both = mm(patch, jnp.concatenate(right, axis=1))
    high, low = split(both[:, :PATCH] + both[:, PATCH:])
    lower = jnp.concatenate([high, jnp.zeros_like(low)], axis=1)
    inner = jnp.concatenate([jnp.concatenate([high, low], axis=1), lower], axis=0)
    moved = mm(jnp.concatenate(left, axis=1), inner)
    corner = (rows[2][i : i + 1, :] * checker) * parity
    return (moved[:, :PATCH] + moved[:, PATCH:]) - corner


def total(value):
    return jnp.sum(jnp.sum(value, axis=0, keepdims=True), axis=1, keepdims=True)


def term_rows(d_rows, d_cols):
    both = jnp.concatenate([d_rows, d_cols], axis=0)
    tangent, signed, peak, whole = shift_terms(both)
    pieces = [t[i : i + 1] for i in range(2) for t in (tangent, signed, peak, whole)]
    return jnp.concatenate(pieces, axis=0)


def patch_slices(width):
    return [slice(i * PATCH, (i + 1) * PATCH) for i in range(width // PATCH)]


def chain_kernel(
    tile_count,
    grid_cols,
    offsets_in,
    mask_in,
    left_in,
    right_in,
    window_in,
    strip,
    out_ref,
    left_ref,
    right_ref,
    window,
    offsets,
    mask_ref,
    load_sem,
    own_raw,
    prev_raw,
    next_raw,
    own_re,
    own_im,
    down_cross,
    up_cross,
    stats,
    mask_tile,
    mask_slots,
    flow_tile,
    flow_slots,
    shift_ref,
    bulk_send,
    bulk_recv,
    mask_send,
    mask_recv,
    flow_send,
    flow_recv,
):
    per_section = tile_count // SECTIONS
    me = lax.axis_index("tile")
    lead = per_section // 2
    rotated = lax.rem(me + tile_count - lead, tile_count)
    group = rotated // per_section
    row = lax.rem(rotated, per_section)
    chunks, width = own_raw.shape[0], own_raw.shape[2]
    pair = width // PATCH
    nodes = chunks * pair
    half = lax.rem(group, 2)
    base = half * nodes

    def device(section, line):
        return lax.rem(section * per_section + line + lead, tile_count)

    def mate(line_step):
        return lax.rem(row + line_step, per_section)

    barrier = pltpu.get_barrier_semaphore()
    for step in range(1, tile_count):
        peer = lax.rem(me + step, tile_count)
        pl.semaphore_signal(barrier, inc=1, device_id={"tile": peer}, device_id_type=MESH)

    def columns(side, chunk):
        start = pl.multiple_of((side * chunks + chunk) * width, LANES)
        return strip.at[:, pl.ds(start, width)]

    loads = [
        pltpu.make_async_copy(source, target, load_sem.at[i])
        for i, (source, target) in enumerate(
            [(mask_in, mask_ref), (offsets_in, offsets), (window_in, window)]
            + [(left_in, left_ref), (right_in, right_ref)]
            + [(columns(half, q), own_raw.at[q]) for q in range(chunks)]
        )
    ]
    for copy in loads:
        copy.start()
    loads[0].wait()
    shape = (2 * per_section, LANES)
    sub = lax.broadcasted_iota(jnp.int32, shape, 0)
    lane = lax.broadcasted_iota(jnp.int32, shape, 1)
    sub_row = lax.rem(sub, per_section)
    mask_tile[...] = jnp.zeros(shape, f32)
    mask_tile[0:1, 0:grid_cols] = mask_ref[...].astype(f32)
    mask_row = mask_tile[0:1, :]
    mask_tile[...] = jnp.where(sub_row == row, mask_row, 0.0)
    mask_slots[1, row] = mask_tile[...]
    shift_ref[...] = jnp.zeros((2,) + shape, f32)

    pl.semaphore_wait(barrier, tile_count - 1)

    def bulk(way, chunk):
        peer = lax.rem(me + (per_section if way else tile_count - per_section), tile_count)
        return pltpu.make_async_remote_copy(
            src_ref=columns(1 - half, chunk),
            dst_ref=(prev_raw if way else next_raw).at[chunk],
            send_sem=bulk_send.at[way, chunk],
            recv_sem=bulk_recv.at[1 - way, chunk],
            device_id={"tile": peer},
            device_id_type=MESH,
        )

    def start_bulk(way):
        for chunk in range(chunks):
            bulk(way, chunk).start()

    def end_bulk(way):
        for chunk in range(chunks):
            bulk(way, chunk).wait_send()

    @pl.when(jnp.logical_or(group == 1, group == 2))
    def _():
        start_bulk(0)

    @pl.when(group <= 1)
    def _():
        start_bulk(1)

    def mask_copy(ahead, step):
        return pltpu.make_async_remote_copy(
            src_ref=mask_tile,
            dst_ref=mask_slots.at[1 - ahead, row],
            send_sem=mask_send.at[ahead, step],
            recv_sem=mask_recv.at[1 - ahead, row],
            device_id={"tile": device(group + ahead, mate(step))},
            device_id_type=MESH,
        )

    for step in range(1, per_section):
        mask_copy(0, step).start()

    @pl.when(group < SECTIONS - 1)
    def _():
        for step in range(per_section):
            mask_copy(1, step).start()

    for copy in loads[1:]:
        copy.wait()

    eight = lax.broadcasted_iota(jnp.int32, (8, LANES), 0)

    def spectra(pixels, kind, first_node):
        table = left_ref[...]
        first = mm(table, jnp.concatenate([pixels, pixels], axis=0))
        found = []
        for i in range(pair):
            s = slice(i * PATCH, (i + 1) * PATCH)
            level = jnp.sum(first[0:1, s], axis=1, keepdims=True) * (1.0 / PATCH)
            top = jnp.where(eight == 0, first[0:8, s] - level, first[0:8, s])
            body = jnp.concatenate([top, first[8:PATCH, s]], axis=0)
            halves = jnp.concatenate([body, first[PATCH:, s]], axis=1).astype(bf16)
            both = mm(halves, right_ref[...])
            real, imag = both[:, :PATCH], both[:, PATCH:]
            energy = real * real + imag * imag
            middle = slice(PATCH // 2, PATCH // 2 + 1)
            node = first_node + i
            stats[kind, 0, node : node + 1] = jnp.sum(energy, axis=0, keepdims=True)
            stats[kind, 1, node : node + 1] = energy[middle]
            stats[kind, 2, node : node + 1] = real[middle]
            found.append((real, imag))
        return found

    def cross(a, b):
        real = a[0] * b[0] + a[1] * b[1]
        imag = a[1] * b[0] - a[0] * b[1]
        return jnp.concatenate([real, imag], axis=1).astype(bf16)

    for q in range(chunks):
        for i, (real, imag) in enumerate(spectra(own_raw[q], 0, q * pair)):
            own_re[q * pair + i] = real
            own_im[q * pair + i] = imag

    def arrived(way, chunk):
        buffer = (next_raw if way else prev_raw).at[chunk]
        pltpu.make_async_copy(buffer, buffer, bulk_recv.at[way, chunk]).wait()

    def own(node):
        return own_re[node], own_im[node]

    up_ok = (sub_row > 0).astype(f32)
    down_ok = (sub_row < per_section - 1).astype(f32)
    left_ok = jnp.logical_and(lane > 0, lane < grid_cols).astype(f32)
    right_ok = (lane < grid_cols - 1).astype(f32)
    count = up_ok + down_ok + left_ok + right_ok

    def relax(flow, mask):
        weight = anchor_weight * mask
        pull = weight * flow
        scale = 1.0 / (weight + count)
        d = flow * mask
        for _ in range(SWEEPS):
            near = (
                up_ok * pltpu.roll(d, 1, 0)
                + down_ok * pltpu.roll(d, 2 * per_section - 1, 0)
                + left_ok * pltpu.roll(d, 1, 1)
                + right_ok * pltpu.roll(d, LANES - 1, 1)
            )
            d = (pull + near) * scale
        return jnp.where(lane < grid_cols, d, 0.0)

    node_sub = lax.broadcasted_iota(jnp.int32, (nodes, LANES), 0)
    node_lane = lax.broadcasted_iota(jnp.int32, (nodes, LANES), 1)
    diagonal = node_lane == base + node_sub
    nyquist = node_lane == PATCH // 2
    frequency = jnp.where(node_lane < PATCH // 2, node_lane, node_lane - PATCH).astype(f32)
    frequency = frequency * (1.0 / PATCH)
    corr_row = lax.broadcasted_iota(jnp.int32, (PADDED, PADDED), 0)
    corr_col = lax.broadcasted_iota(jnp.int32, (PADDED, PADDED), 1)
    inside = jnp.logical_and(corr_row < WINDOW, corr_col < WINDOW)
    gather_sub = lax.broadcasted_iota(jnp.int32, (2 * nodes, nodes * PADDED), 0)
    gather_lane = lax.broadcasted_iota(jnp.int32, (2 * nodes, nodes * PADDED), 1)
    middle = slice(PATCH // 2, PATCH // 2 + 1)

    def column(d, which):
        line = jnp.sum(jnp.where(sub == row + which * per_section, d, 0.0), axis=0, keepdims=True)
        return jnp.sum(jnp.where(diagonal, line, 0.0), axis=1, keepdims=True)

    def flows(section, crosses, kind_a, kind_b, d):
        row_offset = offsets[0, section]
        col_offset = offsets[1, section]
        turned = []
        for which in range(2):
            cosine, sine = turn(frequency * column(d, which))
            turned.append((cosine, jnp.where(nyquist, 0.0, sine), cosine[:, middle], sine[:, middle]))
        (cos_y, sin_y, end_cy, end_sy), (cos_x, sin_x, end_cx, end_sx) = turned
        total_a = jnp.sum(stats[kind_a, 0], axis=1, keepdims=True)
        edge_col = stats[kind_b, 0]
        total_b = jnp.sum(edge_col, axis=1, keepdims=True)
        edge_row = jnp.sum(stats[kind_b, 1], axis=1, keepdims=True)
        tip_a = stats[kind_a, 2][:, middle]
        tip_b = stats[kind_b, 2][:, middle]
        tip = tip_b * tip_b
        end_both = end_cy * end_cx - end_sy * end_sx
        lost = (
            (edge_row - tip) * (end_sy * end_sy)
            + (edge_col[:, middle] - tip) * (end_sx * end_sx)
            + tip * (1.0 - end_both * end_both)
        )
        size = 1.0 / float(PATCH) ** 4
        variance_a = total_a * size + 1e-05
        variance_b = jnp.maximum((total_b - lost) * size, 0.0) + 1e-05
        scales = (sharpness * size) * lax.rsqrt(variance_a * variance_b)
        corners = end_sy * end_sx * tip_a * tip_b
        row_cos = window[0, pl.ds(row_offset + REACH, PADDED), :]
        row_sin = window[1, pl.ds(row_offset + REACH, PADDED), :]
        col_cos = window[0, pl.ds(col_offset + REACH, PADDED), :]
        col_sin = window[1, pl.ds(col_offset + REACH, PADDED), :]
        col_high, col_low = split(jnp.concatenate([col_cos, -col_sin], axis=1))
        moved = []
        for i in range(nodes):
            c, s = cos_y[i : i + 1], sin_y[i : i + 1]
            table = jnp.concatenate(
                [row_cos * c + row_sin * s, row_sin * c - row_cos * s], axis=0
            )
            parts = mm(jnp.concatenate(split(table), axis=0), crosses[i])
            parts = parts[: 2 * PADDED] + parts[2 * PADDED :]
            real = parts[:PADDED, :PATCH] - parts[PADDED:, PATCH:]
            imag = parts[:PADDED, PATCH:] + parts[PADDED:, :PATCH]
            c, s = cos_x[i : i + 1], sin_x[i : i + 1]
            moved.append(
                jnp.concatenate([real * c + imag * s, imag * c - real * s], axis=1)
            )
        high, low = split(jnp.concatenate(moved, axis=0))
        correlation = mm_nt(
            jnp.concatenate([high, low, high], axis=1),
            jnp.concatenate([col_high, col_high, col_low], axis=1),
        )
        odd = (corr_row + corr_col + (row_offset + col_offset + 2 * REACH)) & 1
        parity = 1.0 - 2.0 * odd.astype(f32)
        weights = []
        for i in range(nodes):
            here = correlation[i * PADDED : (i + 1) * PADDED] - corners[i : i + 1] * parity
            weights.append(jnp.where(inside, jnp.exp(here * scales[i : i + 1]), 0.0))
        high, low = split(jnp.concatenate(weights, axis=0))
        shifts = (lax.rem(gather_lane, PADDED) - HALF + row_offset).astype(f32)
        gather = jnp.where(gather_sub < nodes, 1.0, shifts)
        block = gather_lane // PADDED == lax.rem(gather_sub, nodes)
        gather = jnp.where(block, gather, 0.0).astype(bf16)
        sums = mm(
            jnp.concatenate([gather, gather], axis=1), jnp.concatenate([high, low], axis=0)
        )
        plain = sums[:nodes]
        across = lax.broadcasted_iota(jnp.int32, (nodes, PADDED), 1) - HALF + col_offset
        inverse = 1.0 / jnp.sum(plain, axis=1, keepdims=True)
        flow_row = jnp.sum(sums[nodes:], axis=1, keepdims=True) * inverse
        flow_col = jnp.sum(plain * across.astype(f32), axis=1, keepdims=True) * inverse
        line_row = jnp.sum(jnp.where(diagonal, flow_row, 0.0), axis=0, keepdims=True)
        line_col = jnp.sum(jnp.where(diagonal, flow_col, 0.0), axis=0, keepdims=True)
        tile = jnp.where(sub == row, line_row, 0.0)
        return jnp.where(sub == row + per_section, line_col, tile)

    def flow_copy(phase, ahead, step):
        part = 1 - phase
        slot = 1 - ahead
        return pltpu.make_async_remote_copy(
            src_ref=flow_tile.at[phase],
            dst_ref=flow_slots.at[slot, part, row],
            send_sem=flow_send.at[phase, ahead, step],
            recv_sem=flow_recv.at[slot, part, row],
            device_id={"tile": device(group + phase + ahead, mate(step))},
            device_id_type=MESH,
        )

    def each_flow(phase, act):
        for step in range(1 - phase, per_section):
            act(flow_copy(phase, 0, step))

        @pl.when(group + phase + 1 < SECTIONS)
        def _():
            for step in range(per_section):
                act(flow_copy(phase, 1, step))

    def take(slots, sems, slot, part, line):
        buffer = slots.at[slot, part, line]
        pltpu.make_async_copy(buffer, buffer, sems.at[slot, part, line]).wait()

    def gathered(slot):
        flow = jnp.zeros(shape, f32)
        mask = jnp.zeros(shape, f32)
        for part in range(2):
            for step in range(1 if slot == 1 and part == 1 else 0, per_section):
                take(flow_slots, flow_recv, slot, part, mate(step))
            for line in range(per_section):
                flow = flow + flow_slots[slot, part, line]
        for line in range(per_section):
            mask = mask + mask_slots[slot, line]
        return relax(flow, mask)

    @pl.when(group >= 1)
    def _():
        for q in range(chunks):
            arrived(0, q)
            if q == 0:

                @pl.when(group == SECTIONS - 1)
                def _():
                    start_bulk(0)

            for i, found in enumerate(spectra(prev_raw[q], 1, q * pair)):
                down_cross[q * pair + i] = cross(own(q * pair + i), found)
        end_bulk(0)

        @pl.when(group == 2)
        def _():
            start_bulk(1)

        for step in range(per_section):
            pltpu.make_async_copy(
                mask_slots.at[0, mate(step)], mask_slots.at[0, mate(step)], mask_recv.at[0, mate(step)]
            ).wait()

        @pl.when(group >= 2)
        def _():
            shift_ref[0] = gathered(0)

        tile = flows(group, down_cross, 0, 1, shift_ref[0])
        flow_tile[0] = tile
        flow_slots[1, 1, row] = tile
        each_flow(0, lambda copy: copy.start())

    @pl.when(group < SECTIONS - 1)
    def _():
        for q in range(chunks):
            arrived(1, q)
            for i, found in enumerate(spectra(next_raw[q], 2, q * pair)):
                up_cross[q * pair + i] = cross(found, own(q * pair + i))

    for step in range(1, per_section):
        pltpu.make_async_copy(
            mask_slots.at[1, mate(step)], mask_slots.at[1, mate(step)], mask_recv.at[1, mate(step)]
        ).wait()

    @pl.when(group >= 1)
    def _():
        shift_ref[1] = gathered(1)

    @pl.when(group < SECTIONS - 1)
    def _():
        flow_tile[1] = flows(group + 1, up_cross, 2, 0, shift_ref[1])
        each_flow(1, lambda copy: copy.start())

    home = shift_ref[1]
    out_row = jnp.sum(jnp.where(sub == row, home, 0.0), axis=0, keepdims=True)
    out_col = jnp.sum(jnp.where(sub == row + per_section, home, 0.0), axis=0, keepdims=True)
    out_ref[...] = jnp.concatenate([out_row, out_col], axis=0)

    for step in range(1, per_section):
        mask_copy(0, step).wait_send()

    @pl.when(group < SECTIONS - 1)
    def _():
        for step in range(per_section):
            mask_copy(1, step).wait_send()
        end_bulk(1)
        each_flow(1, lambda copy: copy.wait_send())

    @pl.when(group >= 1)
    def _():
        each_flow(0, lambda copy: copy.wait_send())


def warp_kernel(
    shift_ref, strip_in, warp_tables, parity_ref, out, node_ref, strip, result, sems
):
    pieces = strip.shape[0]
    width = strip.shape[2]
    loads, stores = [], []
    for k in range(pieces):
        where = pl.ds(k * width, width)
        loads.append(pltpu.make_async_copy(strip_in.at[:, where], strip.at[k], sems.at[k]))
        stores.append(
            pltpu.make_async_copy(result.at[k], out.at[:, where], sems.at[pieces + k])
        )
        loads[k].start()
    nodes = node_ref.shape[2]
    node_ref[0] = shift_ref[0:1, 0:nodes]
    node_ref[1] = shift_ref[1:2, 0:nodes]
    rows = kernel_rows(term_rows(shift_ref[0:1, :], shift_ref[1:2, :]), warp_tables[...])
    parity = parity_ref[...]
    for k in range(pieces):
        loads[k].wait()
        for j, s in enumerate(patch_slices(width)):
            i = k * (width // PATCH) + j
            patch = strip[k, :, s]
            checker = total(patch.astype(f32) * parity)
            result[k, :, s] = warp_patch(patch, rows, i, checker, parity).astype(bf16)
        stores[k].start()
    for copy in stores:
        copy.wait()


def shards(tile_count, sections, valid_mask, coarse_offsets):
    per_section = tile_count // SECTIONS
    grid_cols = valid_mask.shape[1]
    width = CHUNK * PATCH
    chunks = sections.shape[1] // (2 * width)
    nodes = chunks * CHUNK
    tile_shape = (2 * per_section, LANES)
    vmem = pl.BlockSpec(memory_space=pltpu.VMEM)
    left, right, window, warp_tables, parity = constants()
    hbm = pl.BlockSpec(memory_space=pltpu.HBM)
    raw = pltpu.VMEM((chunks, PATCH, width), bf16)
    spectrum = pltpu.VMEM((nodes, PATCH, PATCH), f32)
    crossed = pltpu.VMEM((nodes, PATCH, 2 * PATCH), bf16)
    dma = pltpu.SemaphoreType.DMA
    shift = pl.pallas_call(
        functools.partial(chain_kernel, tile_count, grid_cols),
        out_shape=jax.ShapeDtypeStruct((2, LANES), f32),
        in_specs=[hbm] * 6,
        out_specs=vmem,
        scratch_shapes=[
            pltpu.VMEM(left.shape, bf16),
            pltpu.VMEM(right.shape, bf16),
            pltpu.VMEM(window.shape, f32),
            pltpu.SMEM(coarse_offsets.shape[::-1], jnp.int32),
            pltpu.VMEM(valid_mask.shape, jnp.int32),
            dma((5 + chunks,)),
            raw,
            raw,
            raw,
            spectrum,
            spectrum,
            crossed,
            crossed,
            pltpu.VMEM((3, 3, nodes, LANES), f32),
            pltpu.VMEM(tile_shape, f32),
            pltpu.VMEM((2, per_section) + tile_shape, f32),
            pltpu.VMEM((2,) + tile_shape, f32),
            pltpu.VMEM((2, 2, per_section) + tile_shape, f32),
            pltpu.VMEM((2,) + tile_shape, f32),
            dma((2, chunks)),
            dma((2, chunks)),
            dma((2, per_section)),
            dma((2, per_section)),
            dma((2, 2, per_section)),
            dma((2, 2, per_section)),
        ],
        compiler_params=pltpu.CompilerParams(
            collective_id=0, has_side_effects=True
        ),
        name="chain",
    )(coarse_offsets.T, valid_mask, left, right, window, sections)
    return pl.pallas_call(
        warp_kernel,
        out_shape=(
            jax.ShapeDtypeStruct(sections.shape, bf16),
            jax.ShapeDtypeStruct((2, 1, grid_cols), f32),
        ),
        in_specs=[vmem, hbm, vmem, vmem],
        out_specs=(hbm, vmem),
        scratch_shapes=[
            pltpu.VMEM((PIECES, PATCH, sections.shape[1] // PIECES), bf16),
            pltpu.VMEM((PIECES, PATCH, sections.shape[1] // PIECES), bf16),
            pltpu.SemaphoreType.DMA((2 * PIECES,)),
        ],
        name="warp",
    )(shift, sections, warp_tables, parity)


def solution(mesh):
    placed = (P(("parts", "tile"), None), P(("parts", "tile"), None), P("parts", None))
    return jax.shard_map(
        functools.partial(shards, mesh.shape["tile"]),
        mesh=mesh,
        in_specs=placed,
        out_specs=(P(("parts", "tile"), None), P(None, ("parts", "tile"), None)),
        check_vma=False,
    )
```

time: 45.2 us -> 37.9 us (0.84)
  Pallas kernels: 44.3 us -> 37.1 us
    pallas_call x1, Pallas kernels: 39.9 us -> 32.6 us  [shards(): pl.pallas_call(functools.partial(chain_kernel, tile_count, grid_cols), ou...]
where the time goes in v1:
time: 37.9 us; the launch traced here: 37.7 us
  Pallas kernels  37.1 us (98%)
  between operations  0.64 us (2%)
    pallas_call x1, Pallas kernels, shards(): pl.pallas_call(functools.partial(chain_kernel, tile_count, grid_cols), ou...  32.6 us
    pallas_call x1, Pallas kernels, shards(): pl.pallas_call(warp_kernel, out_shape=(jax.ShapeDtypeStruct(sections.shap...  4.49 us

profile of v1, /device:TPU:0, one launch (start us, length us, event | category | flops | bytes accessed | tf_op | source)
XLA Modules:
  0.0 37.7 jit_solution(5173974040185663282)
XLA Ops:
  0.6 32.6 %chain.1.shift_ref = f32[2,128]{1,0:T(2,128)} custom-call(s32[2,4]{1,0:T(2,128)} %bitcast.1, s32[1,16]{1,0:T(1,128)} %mask_in.1, bf16[256,256]{1,0:T(8,128)(2,1)} %constant.10.clone.left_in, bf16[256,256]{1,0:T(8,128)(2,1)} %constant.11.clone.right_in, f32[2,24,128]{2,1,0:T(8,128)} %constant.12.clone.window_in, bf16[128,2048]{1,0:T(8,128)(2,1)} %strip_in.1), custom_call_target="tpu_custom_call" | custom-call | tf_op jit(solution)/shard_map/chain/pallas_call | solution.py:585
  33.2 4.5 %warp.1 = (bf16[128,2048]{1,0:T(8,128)(2,1)}, f32[2,1,16]{2,1,0:T(1,128)}) custom-call(f32[2,128]{1,0:T(2,128)} %chain.1.shift_ref, bf16[128,2048]{1,0:T(8,128)(2,1)} %strip_in.1, f32[8,128]{1,0:T(8,128)} %constant.13.clone.warp_tables, f32[128,128]{1,0:T(8,128)} %constant.14.clone.parity_ref), custom_call_target="tpu_custom_call" | custom-call | tf_op jit(solution)/shard_map/warp/pallas_call | solution.py:622

commit v2 on v1

--- a/solution.py
+++ b/solution.py
@@ -17,6 +17,8 @@
 PADDED = 16
 LANES = 128
 CHUNK = 2
+PACE = 2900
+REST = 1500
 PIECES = 2
 
 sharpness = 12.0
@@ -176,6 +178,10 @@
     mask_recv,
     flow_send,
     flow_recv,
+    go_sem,
+    relay_raw,
+    relay_send,
+    relay_recv,
 ):
     per_section = tile_count // SECTIONS
     me = lax.axis_index("tile")
@@ -239,9 +245,46 @@
             device_id_type=MESH,
         )
 
-    def start_bulk(way):
-        for chunk in range(chunks):
+    def start_bulk(way, first=0, last=chunks):
+        for chunk in range(first, last):
             bulk(way, chunk).start()
+
+    straight = chunks // 2
+    apart = per_section - per_section // 2
+    wrapped = row >= apart
+
+    def detour(way):
+        for k in range(chunks - straight):
+            pltpu.make_async_remote_copy(
+                src_ref=columns(1 - half, straight + k),
+                dst_ref=relay_raw.at[k],
+                send_sem=bulk_send.at[way, straight + k],
+                recv_sem=relay_recv.at[k],
+                device_id={"tile": device(SECTIONS - 1 if way else 0, row - apart)},
+                device_id_type=MESH,
+            ).start()
+
+    def onward(way, k):
+        return pltpu.make_async_remote_copy(
+            src_ref=relay_raw.at[k],
+            dst_ref=(prev_raw if way else next_raw).at[straight + k],
+            send_sem=relay_send.at[k],
+            recv_sem=bulk_recv.at[1 - way, straight + k],
+            device_id={"tile": device(SECTIONS - 1 if way else 2, row + apart)},
+            device_id_type=MESH,
+        )
+
+    def forward(way, k):
+        pltpu.make_async_copy(relay_raw.at[k], relay_raw.at[k], relay_recv.at[k]).wait()
+        onward(way, k).start()
+
+    def release():
+        pl.semaphore_signal(
+            go_sem,
+            inc=1,
+            device_id={"tile": device(SECTIONS - 1, row)},
+            device_id_type=MESH,
+        )
 
     def end_bulk(way):
         for chunk in range(chunks):
@@ -254,6 +297,17 @@
     @pl.when(group <= 1)
     def _():
         start_bulk(1)
+
+    for way in range(2):
+        mine = group == SECTIONS - 1 - way
+
+        @pl.when(jnp.logical_and(mine, wrapped))
+        def _():
+            detour(way)
+
+        @pl.when(jnp.logical_and(mine, jnp.logical_not(wrapped)))
+        def _():
+            start_bulk(way)
 
     def mask_copy(ahead, step):
         return pltpu.make_async_remote_copy(
@@ -465,23 +519,45 @@
             mask = mask + mask_slots[slot, line]
         return relax(flow, mask)
 
+    @pl.when(group == SECTIONS - 1)
+    def _():
+        pl.semaphore_wait(go_sem, 1)
+
+        @pl.when(wrapped)
+        def _():
+            for chunk in range(straight):
+                if chunk:
+                    pl.delay(PACE)
+                bulk(0, chunk).start()
+
+        @pl.when(jnp.logical_not(wrapped))
+        def _():
+            for k in range(chunks - straight):
+                if k:
+                    pl.delay(PACE)
+                forward(1, k)
+
     @pl.when(group >= 1)
     def _():
         for q in range(chunks):
             arrived(0, q)
-            if q == 0:
-
-                @pl.when(group == SECTIONS - 1)
-                def _():
-                    start_bulk(0)
-
             for i, found in enumerate(spectra(prev_raw[q], 1, q * pair)):
                 down_cross[q * pair + i] = cross(own(q * pair + i), found)
-        end_bulk(0)
+
+        @pl.when(group == 1)
+        def _():
+            end_bulk(0)
 
         @pl.when(group == 2)
         def _():
-            start_bulk(1)
+            end_bulk(0)
+
+        @pl.when(jnp.logical_and(group == 2, wrapped))
+        def _():
+            for chunk in range(straight):
+                if chunk:
+                    pl.delay(PACE)
+                bulk(1, chunk).start()
 
         for step in range(per_section):
             pltpu.make_async_copy(
@@ -501,6 +577,17 @@
     def _():
         for q in range(chunks):
             arrived(1, q)
+            if q == chunks - 1:
+
+                @pl.when(group == 0)
+                def _():
+                    release()
+
+                @pl.when(jnp.logical_and(group == 0, jnp.logical_not(wrapped)))
+                def _():
+                    for k in range(chunks - straight - 1):
+                        forward(0, k)
+
             for i, found in enumerate(spectra(next_raw[q], 2, q * pair)):
                 up_cross[q * pair + i] = cross(found, own(q * pair + i))
 
@@ -518,6 +605,11 @@
         flow_tile[1] = flows(group + 1, up_cross, 2, 0, shift_ref[1])
         each_flow(1, lambda copy: copy.start())
 
+        @pl.when(jnp.logical_and(group == 0, jnp.logical_not(wrapped)))
+        def _():
+            pl.delay(REST)
+            forward(0, chunks - straight - 1)
+
     home = shift_ref[1]
     out_row = jnp.sum(jnp.where(sub == row, home, 0.0), axis=0, keepdims=True)
     out_col = jnp.sum(jnp.where(sub == row + per_section, home, 0.0), axis=0, keepdims=True)
@@ -530,12 +622,24 @@
     def _():
         for step in range(per_section):
             mask_copy(1, step).wait_send()
+
         end_bulk(1)
         each_flow(1, lambda copy: copy.wait_send())
 
     @pl.when(group >= 1)
     def _():
         each_flow(0, lambda copy: copy.wait_send())
+
+    @pl.when(group == SECTIONS - 1)
+    def _():
+        end_bulk(0)
+
+    for way, section in ((0, 0), (1, SECTIONS - 1)):
+
+        @pl.when(jnp.logical_and(group == section, jnp.logical_not(wrapped)))
+        def _():
+            for k in range(chunks - straight):
+                onward(way, k).wait_send()
 
 
 def warp_kernel(
@@ -613,6 +717,10 @@
             dma((2, per_section)),
             dma((2, 2, per_section)),
             dma((2, 2, per_section)),
+            pltpu.SemaphoreType.REGULAR,
+            pltpu.VMEM((chunks - chunks // 2, PATCH, width), bf16),
+            dma((chunks - chunks // 2,)),
+            dma((chunks - chunks // 2,)),
         ],
         compiler_params=pltpu.CompilerParams(
             collective_id=0, has_side_effects=True

time: 37.9 us -> 35 us (0.923)
  Pallas kernels: 37.1 us -> 34.1 us
    pallas_call x1, Pallas kernels: 32.6 us -> 29.6 us  [shards(): pl.pallas_call(functools.partial(chain_kernel, tile_count, grid_cols), ou...]
where the time goes in v2:
time: 35 us; the launch traced here: 34.8 us
  Pallas kernels  34.1 us (97%)
  between operations  0.64 us (2%)
    pallas_call x1, Pallas kernels, shards(): pl.pallas_call(functools.partial(chain_kernel, tile_count, grid_cols), ou...  29.6 us
    pallas_call x1, Pallas kernels, shards(): pl.pallas_call(warp_kernel, out_shape=(jax.ShapeDtypeStruct(sections.shap...  4.49 us

profile of v2, /device:TPU:0, one launch (start us, length us, event | category | flops | bytes accessed | tf_op | source)
XLA Modules:
  0.0 34.8 jit_solution(6546639618613367307)
XLA Ops:
  0.6 29.6 %chain.1.shift_ref = f32[2,128]{1,0:T(2,128)} custom-call(s32[2,4]{1,0:T(2,128)} %bitcast.1, s32[1,16]{1,0:T(1,128)} %mask_in.1, bf16[256,256]{1,0:T(8,128)(2,1)} %constant.10.clone.left_in, bf16[256,256]{1,0:T(8,128)(2,1)} %constant.11.clone.right_in, f32[2,24,128]{2,1,0:T(8,128)} %constant.12.clone.window_in, bf16[128,2048]{1,0:T(8,128)(2,1)} %strip_in.1), custom_call_target="tpu_custom_call" | custom-call | tf_op jit(solution)/shard_map/chain/pallas_call | solution.py:689
  30.3 4.5 %warp.1 = (bf16[128,2048]{1,0:T(8,128)(2,1)}, f32[2,1,16]{2,1,0:T(1,128)}) custom-call(f32[2,128]{1,0:T(2,128)} %chain.1.shift_ref, bf16[128,2048]{1,0:T(8,128)(2,1)} %strip_in.1, f32[8,128]{1,0:T(8,128)} %constant.13.clone.warp_tables, f32[128,128]{1,0:T(8,128)} %constant.14.clone.parity_ref), custom_call_target="tpu_custom_call" | custom-call | tf_op jit(solution)/shard_map/warp/pallas_call | solution.py:730

commit v3 on v2

--- a/solution.py
+++ b/solution.py
@@ -17,8 +17,8 @@
 PADDED = 16
 LANES = 128
 CHUNK = 2
-PACE = 2900
-REST = 1500
+HUB = 2
+REST = 2500
 PIECES = 2
 
 sharpness = 12.0
@@ -179,6 +179,7 @@
     flow_send,
     flow_recv,
     go_sem,
+    all_sem,
     relay_raw,
     relay_send,
     relay_recv,
@@ -202,9 +203,26 @@
         return lax.rem(row + line_step, per_section)
 
     barrier = pltpu.get_barrier_semaphore()
-    for step in range(1, tile_count):
-        peer = lax.rem(me + step, tile_count)
-        pl.semaphore_signal(barrier, inc=1, device_id={"tile": peer}, device_id_type=MESH)
+
+    def signal(sem, section, line):
+        pl.semaphore_signal(
+            sem, inc=1, device_id={"tile": device(section, line)}, device_id_type=MESH
+        )
+
+    @pl.when(group <= 1)
+    def _():
+        signal(barrier, 1 - group, row)
+
+    @pl.when(group == HUB)
+    def _():
+        signal(barrier, SECTIONS - 1, row)
+        for step in range(1, per_section):
+            signal(barrier, HUB, mate(step))
+
+    @pl.when(group != HUB)
+    def _():
+        for step in range(per_section):
+            signal(barrier, HUB, mate(step))
 
     def columns(side, chunk):
         start = pl.multiple_of((side * chunks + chunk) * width, LANES)
@@ -220,6 +238,89 @@
     ]
     for copy in loads:
         copy.start()
+    pl.semaphore_wait(barrier, jnp.where(group == HUB, tile_count - 1, 1))
+
+    def bulk(way, chunk):
+        peer = lax.rem(me + (per_section if way else tile_count - per_section), tile_count)
+        return pltpu.make_async_remote_copy(
+            src_ref=columns(1 - half, chunk),
+            dst_ref=(prev_raw if way else next_raw).at[chunk],
+            send_sem=bulk_send.at[way, chunk],
+            recv_sem=bulk_recv.at[1 - way, chunk],
+            device_id={"tile": peer},
+            device_id_type=MESH,
+        )
+
+    def start_bulk(way, first=0, last=chunks):
+        for chunk in range(first, last):
+            bulk(way, chunk).start()
+
+    relayed = (chunks // 2, chunks // 2)
+    apart = per_section - per_section // 2
+    wrapped = row >= apart
+
+    def detour(way):
+        for k in range(relayed[way]):
+            pltpu.make_async_remote_copy(
+                src_ref=columns(1 - half, k),
+                dst_ref=relay_raw.at[k],
+                send_sem=bulk_send.at[way, k],
+                recv_sem=relay_recv.at[k],
+                device_id={"tile": device(SECTIONS - 1 if way else 0, row - apart)},
+                device_id_type=MESH,
+            ).start()
+
+    def onward(way, k):
+        return pltpu.make_async_remote_copy(
+            src_ref=relay_raw.at[k],
+            dst_ref=(prev_raw if way else next_raw).at[k],
+            send_sem=relay_send.at[k],
+            recv_sem=bulk_recv.at[1 - way, k],
+            device_id={"tile": device(SECTIONS - 1 if way else 2, row + apart)},
+            device_id_type=MESH,
+        )
+
+    def forward(way, k):
+        pltpu.make_async_copy(relay_raw.at[k], relay_raw.at[k], relay_recv.at[k]).wait()
+        onward(way, k).start()
+
+    def release():
+        signal(go_sem, SECTIONS - 1, row)
+
+    def end_bulk(way):
+        for chunk in range(chunks):
+            bulk(way, chunk).wait_send()
+
+    @pl.when(group == HUB)
+    def _():
+        for section in range(SECTIONS):
+            if section != HUB:
+                signal(all_sem, section, row)
+
+    @pl.when(jnp.logical_or(group == 1, group == 2))
+    def _():
+        start_bulk(0)
+
+    @pl.when(group == 0)
+    def _():
+        start_bulk(1)
+
+    for way in range(2):
+
+        @pl.when(jnp.logical_and(group == SECTIONS - 1 - way, jnp.logical_not(wrapped)))
+        def _():
+            start_bulk(way)
+
+    def mask_copy(ahead, step):
+        return pltpu.make_async_remote_copy(
+            src_ref=mask_tile,
+            dst_ref=mask_slots.at[1 - ahead, row],
+            send_sem=mask_send.at[ahead, step],
+            recv_sem=mask_recv.at[1 - ahead, row],
+            device_id={"tile": device(group + ahead, mate(step))},
+            device_id_type=MESH,
+        )
+
     loads[0].wait()
     shape = (2 * per_section, LANES)
     sub = lax.broadcasted_iota(jnp.int32, shape, 0)
@@ -231,101 +332,6 @@
     mask_tile[...] = jnp.where(sub_row == row, mask_row, 0.0)
     mask_slots[1, row] = mask_tile[...]
     shift_ref[...] = jnp.zeros((2,) + shape, f32)
-
-    pl.semaphore_wait(barrier, tile_count - 1)
-
-    def bulk(way, chunk):
-        peer = lax.rem(me + (per_section if way else tile_count - per_section), tile_count)
-        return pltpu.make_async_remote_copy(
-            src_ref=columns(1 - half, chunk),
-            dst_ref=(prev_raw if way else next_raw).at[chunk],
-            send_sem=bulk_send.at[way, chunk],
-            recv_sem=bulk_recv.at[1 - way, chunk],
-            device_id={"tile": peer},
-            device_id_type=MESH,
-        )
-
-    def start_bulk(way, first=0, last=chunks):
-        for chunk in range(first, last):
-            bulk(way, chunk).start()
-
-    straight = chunks // 2
-    apart = per_section - per_section // 2
-    wrapped = row >= apart
-
-    def detour(way):
-        for k in range(chunks - straight):
-            pltpu.make_async_remote_copy(
-                src_ref=columns(1 - half, straight + k),
-                dst_ref=relay_raw.at[k],
-                send_sem=bulk_send.at[way, straight + k],
-                recv_sem=relay_recv.at[k],
-                device_id={"tile": device(SECTIONS - 1 if way else 0, row - apart)},
-                device_id_type=MESH,
-            ).start()
-
-    def onward(way, k):
-        return pltpu.make_async_remote_copy(
-            src_ref=relay_raw.at[k],
-            dst_ref=(prev_raw if way else next_raw).at[straight + k],
-            send_sem=relay_send.at[k],
-            recv_sem=bulk_recv.at[1 - way, straight + k],
-            device_id={"tile": device(SECTIONS - 1 if way else 2, row + apart)},
-            device_id_type=MESH,
-        )
-
-    def forward(way, k):
-        pltpu.make_async_copy(relay_raw.at[k], relay_raw.at[k], relay_recv.at[k]).wait()
-        onward(way, k).start()
-
-    def release():
-        pl.semaphore_signal(
-            go_sem,
-            inc=1,
-            device_id={"tile": device(SECTIONS - 1, row)},
-            device_id_type=MESH,
-        )
-
-    def end_bulk(way):
-        for chunk in range(chunks):
-            bulk(way, chunk).wait_send()
-
-    @pl.when(jnp.logical_or(group == 1, group == 2))
-    def _():
-        start_bulk(0)
-
-    @pl.when(group <= 1)
-    def _():
-        start_bulk(1)
-
-    for way in range(2):
-        mine = group == SECTIONS - 1 - way
-
-        @pl.when(jnp.logical_and(mine, wrapped))
-        def _():
-            detour(way)
-
-        @pl.when(jnp.logical_and(mine, jnp.logical_not(wrapped)))
-        def _():
-            start_bulk(way)
-
-    def mask_copy(ahead, step):
-        return pltpu.make_async_remote_copy(
-            src_ref=mask_tile,
-            dst_ref=mask_slots.at[1 - ahead, row],
-            send_sem=mask_send.at[ahead, step],
-            recv_sem=mask_recv.at[1 - ahead, row],
-            device_id={"tile": device(group + ahead, mate(step))},
-            device_id_type=MESH,
-        )
-
-    for step in range(1, per_section):
-        mask_copy(0, step).start()
-
-    @pl.when(group < SECTIONS - 1)
-    def _():
-        for step in range(per_section):
-            mask_copy(1, step).start()
 
     for copy in loads[1:]:
         copy.wait()
@@ -362,6 +368,28 @@
         for i, (real, imag) in enumerate(spectra(own_raw[q], 0, q * pair)):
             own_re[q * pair + i] = real
             own_im[q * pair + i] = imag
+
+    @pl.when(group != HUB)
+    def _():
+        pl.semaphore_wait(all_sem, 1)
+
+    for step in range(1, per_section):
+        mask_copy(0, step).start()
+
+    @pl.when(group < SECTIONS - 1)
+    def _():
+        for step in range(per_section):
+            mask_copy(1, step).start()
+
+    @pl.when(group == 1)
+    def _():
+        start_bulk(1)
+
+    for way in range(2):
+
+        @pl.when(jnp.logical_and(group == SECTIONS - 1 - way, wrapped))
+        def _():
+            detour(way)
 
     def arrived(way, chunk):
         buffer = (next_raw if way else prev_raw).at[chunk]
@@ -521,21 +549,12 @@
 
     @pl.when(group == SECTIONS - 1)
     def _():
-        pl.semaphore_wait(go_sem, 1)
 
         @pl.when(wrapped)
         def _():
-            for chunk in range(straight):
-                if chunk:
-                    pl.delay(PACE)
-                bulk(0, chunk).start()
-
-        @pl.when(jnp.logical_not(wrapped))
-        def _():
-            for k in range(chunks - straight):
-                if k:
-                    pl.delay(PACE)
-                forward(1, k)
+            pl.semaphore_wait(go_sem, 1)
+            start_bulk(0, relayed[0])
+
 
     @pl.when(group >= 1)
     def _():
@@ -554,10 +573,13 @@
 
         @pl.when(jnp.logical_and(group == 2, wrapped))
         def _():
-            for chunk in range(straight):
-                if chunk:
-                    pl.delay(PACE)
-                bulk(1, chunk).start()
+            start_bulk(1, relayed[1])
+
+        @pl.when(jnp.logical_and(group == SECTIONS - 1, jnp.logical_not(wrapped)))
+        def _():
+            for k in range(relayed[1]):
+                forward(1, k)
+
 
         for step in range(per_section):
             pltpu.make_async_copy(
@@ -577,17 +599,6 @@
     def _():
         for q in range(chunks):
             arrived(1, q)
-            if q == chunks - 1:
-
-                @pl.when(group == 0)
-                def _():
-                    release()
-
-                @pl.when(jnp.logical_and(group == 0, jnp.logical_not(wrapped)))
-                def _():
-                    for k in range(chunks - straight - 1):
-                        forward(0, k)
-
             for i, found in enumerate(spectra(next_raw[q], 2, q * pair)):
                 up_cross[q * pair + i] = cross(found, own(q * pair + i))
 
@@ -608,7 +619,12 @@
         @pl.when(jnp.logical_and(group == 0, jnp.logical_not(wrapped)))
         def _():
             pl.delay(REST)
-            forward(0, chunks - straight - 1)
+            for k in range(relayed[0]):
+                forward(0, k)
+
+        @pl.when(jnp.logical_and(group == 0, wrapped))
+        def _():
+            release()
 
     home = shift_ref[1]
     out_row = jnp.sum(jnp.where(sub == row, home, 0.0), axis=0, keepdims=True)
@@ -638,7 +654,7 @@
 
         @pl.when(jnp.logical_and(group == section, jnp.logical_not(wrapped)))
         def _():
-            for k in range(chunks - straight):
+            for k in range(relayed[way]):
                 onward(way, k).wait_send()
 
 
@@ -718,9 +734,10 @@
             dma((2, 2, per_section)),
             dma((2, 2, per_section)),
             pltpu.SemaphoreType.REGULAR,
-            pltpu.VMEM((chunks - chunks // 2, PATCH, width), bf16),
-            dma((chunks - chunks // 2,)),
-            dma((chunks - chunks // 2,)),
+            pltpu.SemaphoreType.REGULAR,
+            raw,
+            dma((chunks,)),
+            dma((chunks,)),
         ],
         compiler_params=pltpu.CompilerParams(
             collective_id=0, has_side_effects=True

time: 35 us -> 32.1 us (0.917)
  Pallas kernels: 34.1 us -> 31.3 us
    pallas_call x1, Pallas kernels: 29.6 us -> 26.8 us  [shards(): pl.pallas_call(functools.partial(chain_kernel, tile_count, grid_cols), ou...]
where the time goes in v3:
time: 32.1 us; the launch traced here: 31.9 us
  Pallas kernels  31.3 us (98%)
  between operations  0.64 us (2%)
    pallas_call x1, Pallas kernels, shards(): pl.pallas_call(functools.partial(chain_kernel, tile_count, grid_cols), ou...  26.8 us
    pallas_call x1, Pallas kernels, shards(): pl.pallas_call(warp_kernel, out_shape=(jax.ShapeDtypeStruct(sections.shap...  4.49 us

profile of v3, /device:TPU:0, one launch (start us, length us, event | category | flops | bytes accessed | tf_op | source)
XLA Modules:
  0.0 31.9 jit_solution(8494596615490826402)
XLA Ops:
  0.6 26.8 %chain.1.shift_ref = f32[2,128]{1,0:T(2,128)} custom-call(s32[2,4]{1,0:T(2,128)} %bitcast.1, s32[1,16]{1,0:T(1,128)} %mask_in.1, bf16[256,256]{1,0:T(8,128)(2,1)} %constant.10.clone.left_in, bf16[256,256]{1,0:T(8,128)(2,1)} %constant.11.clone.right_in, f32[2,24,128]{2,1,0:T(8,128)} %constant.12.clone.window_in, bf16[128,2048]{1,0:T(8,128)(2,1)} %strip_in.1), custom_call_target="tpu_custom_call" | custom-call | tf_op jit(solution)/shard_map/chain/pallas_call | solution.py:705
  27.4 4.5 %warp.1 = (bf16[128,2048]{1,0:T(8,128)(2,1)}, f32[2,1,16]{2,1,0:T(1,128)}) custom-call(f32[2,128]{1,0:T(2,128)} %chain.1.shift_ref, bf16[128,2048]{1,0:T(8,128)(2,1)} %strip_in.1, f32[8,128]{1,0:T(8,128)} %constant.13.clone.warp_tables, f32[128,128]{1,0:T(8,128)} %constant.14.clone.parity_ref), custom_call_target="tpu_custom_call" | custom-call | tf_op jit(solution)/shard_map/warp/pallas_call | solution.py:747

commit v4 on v3

--- a/solution.py
+++ b/solution.py
@@ -92,8 +92,8 @@
     return tangent, signed, peak, whole
 
 
-def kernel_rows(terms, tables):
-    columns = jnp.transpose(terms)[:LANES]
+def kernel_rows(terms, tables, patches):
+    columns = jnp.transpose(terms)[:patches]
     sine, cosine, parity, gap = [tables[i : i + 1, :] for i in range(4)]
     found = []
     for base, forward in ((0, False), (4, True)):
@@ -116,20 +116,15 @@
     return split(pltpu.roll(spread, 0, 1, stride=1, stride_axis=0))
 
 
-def warp_patch(patch, rows, i, checker, parity):
-    left = circulant(rows[0][i : i + 1, :])
-    right = circulant(rows[1][i : i + 1, :])
+def warp_patch(patch, left_row, right_row):
+    left = circulant(left_row)
+    right = circulant(right_row)
     both = mm(patch, jnp.concatenate(right, axis=1))
     high, low = split(both[:, :PATCH] + both[:, PATCH:])
     lower = jnp.concatenate([high, jnp.zeros_like(low)], axis=1)
     inner = jnp.concatenate([jnp.concatenate([high, low], axis=1), lower], axis=0)
     moved = mm(jnp.concatenate(left, axis=1), inner)
-    corner = (rows[2][i : i + 1, :] * checker) * parity
-    return (moved[:, :PATCH] + moved[:, PATCH:]) - corner
-
-
-def total(value):
-    return jnp.sum(jnp.sum(value, axis=0, keepdims=True), axis=1, keepdims=True)
+    return moved[:, :PATCH] + moved[:, PATCH:]
 
 
 def term_rows(d_rows, d_cols):
@@ -137,10 +132,6 @@
     tangent, signed, peak, whole = shift_terms(both)
     pieces = [t[i : i + 1] for i in range(2) for t in (tangent, signed, peak, whole)]
     return jnp.concatenate(pieces, axis=0)
-
-
-def patch_slices(width):
-    return [slice(i * PATCH, (i + 1) * PATCH) for i in range(width // PATCH)]
 
 
 def chain_kernel(
@@ -151,11 +142,18 @@
     left_in,
     right_in,
     window_in,
+    warp_in,
+    parity_in,
     strip,
-    out_ref,
+    out,
+    node_ref,
     left_ref,
     right_ref,
     window,
+    warp_tables,
+    parity_ref,
+    whole,
+    check,
     offsets,
     mask_ref,
     load_sem,
@@ -195,6 +193,8 @@
     nodes = chunks * pair
     half = lax.rem(group, 2)
     base = half * nodes
+    piece = whole.shape[2]
+    patches = PIECES * piece // PATCH
 
     def device(section, line):
         return lax.rem(section * per_section + line + lead, tile_count)
@@ -233,7 +233,9 @@
         for i, (source, target) in enumerate(
             [(mask_in, mask_ref), (offsets_in, offsets), (window_in, window)]
             + [(left_in, left_ref), (right_in, right_ref)]
+            + [(warp_in, warp_tables), (parity_in, parity_ref)]
             + [(columns(half, q), own_raw.at[q]) for q in range(chunks)]
+            + [(strip.at[:, pl.ds(k * piece, piece)], whole.at[k]) for k in range(PIECES)]
         )
     ]
     for copy in loads:
@@ -333,7 +335,7 @@
     mask_slots[1, row] = mask_tile[...]
     shift_ref[...] = jnp.zeros((2,) + shape, f32)
 
-    for copy in loads[1:]:
+    for copy in loads[1:-PIECES]:
         copy.wait()
 
     eight = lax.broadcasted_iota(jnp.int32, (8, LANES), 0)
@@ -602,6 +604,17 @@
             for i, found in enumerate(spectra(next_raw[q], 2, q * pair)):
                 up_cross[q * pair + i] = cross(found, own(q * pair + i))
 
+    def part(i):
+        k, j = divmod(i, piece // PATCH)
+        return whole[k, :, j * PATCH : (j + 1) * PATCH]
+
+    for copy in loads[-PIECES:]:
+        copy.wait()
+    for i in range(patches):
+        check[i : i + 1] = jnp.sum(part(i).astype(f32) * parity_ref[...], axis=0, keepdims=True)
+    sums = jnp.sum(check[...], axis=1, keepdims=True)
+    check[...] = jnp.broadcast_to(sums, check.shape)
+
     for step in range(1, per_section):
         pltpu.make_async_copy(
             mask_slots.at[1, mate(step)], mask_slots.at[1, mate(step)], mask_recv.at[1, mate(step)]
@@ -627,9 +640,21 @@
             release()
 
     home = shift_ref[1]
-    out_row = jnp.sum(jnp.where(sub == row, home, 0.0), axis=0, keepdims=True)
-    out_col = jnp.sum(jnp.where(sub == row + per_section, home, 0.0), axis=0, keepdims=True)
-    out_ref[...] = jnp.concatenate([out_row, out_col], axis=0)
+    lines = [
+        jnp.sum(jnp.where(sub == row + which * per_section, home, 0.0), axis=0, keepdims=True)
+        for which in range(2)
+    ]
+    for which in range(2):
+        node_ref[which] = lines[which][:, :grid_cols]
+    rows = kernel_rows(term_rows(lines[0], lines[1]), warp_tables[...], patches)
+    corner = rows[2] * check[:, 0:1]
+    for k in range(PIECES):
+        for j in range(piece // PATCH):
+            i = k * (piece // PATCH) + j
+            moved = warp_patch(part(i), rows[0][i : i + 1], rows[1][i : i + 1])
+            out[:, i * PATCH : (i + 1) * PATCH] = (
+                moved - corner[i : i + 1] * parity_ref[...]
+            ).astype(bf16)
 
     for step in range(1, per_section):
         mask_copy(0, step).wait_send()
@@ -658,32 +683,13 @@
                 onward(way, k).wait_send()
 
 
-def warp_kernel(
-    shift_ref, strip_in, warp_tables, parity_ref, out, node_ref, strip, result, sems
-):
-    pieces = strip.shape[0]
-    width = strip.shape[2]
-    loads, stores = [], []
-    for k in range(pieces):
-        where = pl.ds(k * width, width)
-        loads.append(pltpu.make_async_copy(strip_in.at[:, where], strip.at[k], sems.at[k]))
-        stores.append(
-            pltpu.make_async_copy(result.at[k], out.at[:, where], sems.at[pieces + k])
-        )
-        loads[k].start()
-    nodes = node_ref.shape[2]
-    node_ref[0] = shift_ref[0:1, 0:nodes]
-    node_ref[1] = shift_ref[1:2, 0:nodes]
-    rows = kernel_rows(term_rows(shift_ref[0:1, :], shift_ref[1:2, :]), warp_tables[...])
-    parity = parity_ref[...]
-    for k in range(pieces):
-        loads[k].wait()
-        for j, s in enumerate(patch_slices(width)):
-            i = k * (width // PATCH) + j
-            patch = strip[k, :, s]
-            checker = total(patch.astype(f32) * parity)
-            result[k, :, s] = warp_patch(patch, rows, i, checker, parity).astype(bf16)
-        stores[k].start()
+def store_kernel(aligned, shift, out, shift_out, sems):
+    stores = [
+        pltpu.make_async_copy(shift, shift_out, sems.at[0]),
+        pltpu.make_async_copy(aligned, out, sems.at[1]),
+    ]
+    for copy in stores:
+        copy.start()
     for copy in stores:
         copy.wait()
 
@@ -702,18 +708,27 @@
     spectrum = pltpu.VMEM((nodes, PATCH, PATCH), f32)
     crossed = pltpu.VMEM((nodes, PATCH, 2 * PATCH), bf16)
     dma = pltpu.SemaphoreType.DMA
-    shift = pl.pallas_call(
+    patches = sections.shape[1] // PATCH
+    pieces = pltpu.VMEM((PIECES, PATCH, sections.shape[1] // PIECES), bf16)
+    aligned, shift = pl.pallas_call(
         functools.partial(chain_kernel, tile_count, grid_cols),
-        out_shape=jax.ShapeDtypeStruct((2, LANES), f32),
-        in_specs=[hbm] * 6,
-        out_specs=vmem,
+        out_shape=(
+            pltpu.VMEM(sections.shape, bf16),
+            pltpu.VMEM((2, 1, grid_cols), f32),
+        ),
+        in_specs=[hbm] * 8,
+        out_specs=(vmem, vmem),
         scratch_shapes=[
             pltpu.VMEM(left.shape, bf16),
             pltpu.VMEM(right.shape, bf16),
             pltpu.VMEM(window.shape, f32),
+            pltpu.VMEM(warp_tables.shape, f32),
+            pltpu.VMEM(parity.shape, f32),
+            pieces,
+            pltpu.VMEM((patches, LANES), f32),
             pltpu.SMEM(coarse_offsets.shape[::-1], jnp.int32),
             pltpu.VMEM(valid_mask.shape, jnp.int32),
-            dma((5 + chunks,)),
+            dma((7 + chunks + PIECES,)),
             raw,
             raw,
             raw,
@@ -743,22 +758,18 @@
             collective_id=0, has_side_effects=True
         ),
         name="chain",
-    )(coarse_offsets.T, valid_mask, left, right, window, sections)
+    )(coarse_offsets.T, valid_mask, left, right, window, warp_tables, parity, sections)
     return pl.pallas_call(
-        warp_kernel,
+        store_kernel,
         out_shape=(
             jax.ShapeDtypeStruct(sections.shape, bf16),
             jax.ShapeDtypeStruct((2, 1, grid_cols), f32),
         ),
-        in_specs=[vmem, hbm, vmem, vmem],
-        out_specs=(hbm, vmem),
-        scratch_shapes=[
-            pltpu.VMEM((PIECES, PATCH, sections.shape[1] // PIECES), bf16),
-            pltpu.VMEM((PIECES, PATCH, sections.shape[1] // PIECES), bf16),
-            pltpu.SemaphoreType.DMA((2 * PIECES,)),
-        ],
-        name="warp",
-    )(shift, sections, warp_tables, parity)
+        in_specs=[vmem, vmem],
+        out_specs=(hbm, hbm),
+        scratch_shapes=[dma((2,))],
+        name="store",
+    )(*[pltpu.with_memory_space_constraint(x, pltpu.VMEM) for x in (aligned, shift)])
 
 
 def solution(mesh):

time: 32.1 us -> 29.3 us (0.913)
  Pallas kernels: 31.3 us -> 28.5 us
    pallas_call x1, Pallas kernels: 4.49 us -> 0.82 us  [shards(): pl.pallas_call(store_kernel, out_shape=(jax.ShapeDtypeStruct(sections.sha...]
    pallas_call x1, Pallas kernels: 26.8 us -> 27.7 us  [shards(): pl.pallas_call(functools.partial(chain_kernel, tile_count, grid_cols), ou...]
where the time goes in v4:
time: 29.3 us; the launch traced here: 29.2 us
  Pallas kernels  28.5 us (97%)
  between operations  0.64 us (2%)
    pallas_call x1, Pallas kernels, shards(): pl.pallas_call(functools.partial(chain_kernel, tile_count, grid_cols), ou...  27.7 us
    pallas_call x1, Pallas kernels, shards(): pl.pallas_call(store_kernel, out_shape=(jax.ShapeDtypeStruct(sections.sha...  0.82 us

profile of v4, /device:TPU:0, one launch (start us, length us, event | category | flops | bytes accessed | tf_op | source)
XLA Modules:
  0.0 29.2 jit_solution(11314875497586981002)
XLA Ops:
  0.6 27.7 %chain.1 = (bf16[128,2048]{1,0:T(8,128)(2,1)S(1)}, f32[2,1,16]{2,1,0:T(1,128)S(1)}) custom-call(s32[2,4]{1,0:T(2,128)} %bitcast.1, s32[1,16]{1,0:T(1,128)} %mask_in.1, bf16[256,256]{1,0:T(8,128)(2,1)} %constant.10.clone.left_in, bf16[256,256]{1,0:T(8,128)(2,1)} %constant.11.clone.right_in, f32[2,24,128]{2,1,0:T(8,128)} %constant.12.clone.window_in, ...), custom_call_target="tpu_custom_call" | custom-call | tf_op jit(solution)/shard_map/chain/pallas_call | solution.py:713
  28.3 0.8 %store.1 = (bf16[128,2048]{1,0:T(8,128)(2,1)}, f32[2,1,16]{2,1,0:T(1,128)}) custom-call(bf16[128,2048]{1,0:T(8,128)(2,1)S(1)} %get-tuple-element.4.aligned, f32[2,1,16]{2,1,0:T(1,128)S(1)} %get-tuple-element.5.shift), custom_call_target="tpu_custom_call" | custom-call | tf_op jit(solution)/shard_map/store/pallas_call | solution.py:762

commit v5 on v4

--- a/solution.py
+++ b/solution.py
@@ -371,6 +371,17 @@
             own_re[q * pair + i] = real
             own_im[q * pair + i] = imag
 
+    def part(i):
+        k, j = divmod(i, piece // PATCH)
+        return whole[k, :, j * PATCH : (j + 1) * PATCH]
+
+    for copy in loads[-PIECES:]:
+        copy.wait()
+    for i in range(patches):
+        check[i : i + 1] = jnp.sum(part(i).astype(f32) * parity_ref[...], axis=0, keepdims=True)
+    sums = jnp.sum(check[...], axis=1, keepdims=True)
+    check[...] = jnp.broadcast_to(sums, check.shape)
+
     @pl.when(group != HUB)
     def _():
         pl.semaphore_wait(all_sem, 1)
@@ -533,11 +544,16 @@
             for step in range(per_section):
                 act(flow_copy(phase, 1, step))
 
-    def take(slots, sems, slot, part, line):
-        buffer = slots.at[slot, part, line]
-        pltpu.make_async_copy(buffer, buffer, sems.at[slot, part, line]).wait()
+    def take(slots, sems, *where):
+        buffer = slots.at[where]
+        pltpu.make_async_copy(buffer, buffer, sems.at[where]).wait()
+
+    def masks(slot):
+        for step in range(slot, per_section):
+            take(mask_slots, mask_recv, slot, mate(step))
 
     def gathered(slot):
+        masks(slot)
         flow = jnp.zeros(shape, f32)
         mask = jnp.zeros(shape, f32)
         for part in range(2):
@@ -565,14 +581,6 @@
             for i, found in enumerate(spectra(prev_raw[q], 1, q * pair)):
                 down_cross[q * pair + i] = cross(own(q * pair + i), found)
 
-        @pl.when(group == 1)
-        def _():
-            end_bulk(0)
-
-        @pl.when(group == 2)
-        def _():
-            end_bulk(0)
-
         @pl.when(jnp.logical_and(group == 2, wrapped))
         def _():
             start_bulk(1, relayed[1])
@@ -582,11 +590,6 @@
             for k in range(relayed[1]):
                 forward(1, k)
 
-
-        for step in range(per_section):
-            pltpu.make_async_copy(
-                mask_slots.at[0, mate(step)], mask_slots.at[0, mate(step)], mask_recv.at[0, mate(step)]
-            ).wait()
 
         @pl.when(group >= 2)
         def _():
@@ -603,22 +606,6 @@
             arrived(1, q)
             for i, found in enumerate(spectra(next_raw[q], 2, q * pair)):
                 up_cross[q * pair + i] = cross(found, own(q * pair + i))
-
-    def part(i):
-        k, j = divmod(i, piece // PATCH)
-        return whole[k, :, j * PATCH : (j + 1) * PATCH]
-
-    for copy in loads[-PIECES:]:
-        copy.wait()
-    for i in range(patches):
-        check[i : i + 1] = jnp.sum(part(i).astype(f32) * parity_ref[...], axis=0, keepdims=True)
-    sums = jnp.sum(check[...], axis=1, keepdims=True)
-    check[...] = jnp.broadcast_to(sums, check.shape)
-
-    for step in range(1, per_section):
-        pltpu.make_async_copy(
-            mask_slots.at[1, mate(step)], mask_slots.at[1, mate(step)], mask_recv.at[1, mate(step)]
-        ).wait()
 
     @pl.when(group >= 1)
     def _():
@@ -656,6 +643,14 @@
                 moved - corner[i : i + 1] * parity_ref[...]
             ).astype(bf16)
 
+    @pl.when(group == 0)
+    def _():
+        masks(1)
+
+    @pl.when(group == 1)
+    def _():
+        masks(0)
+
     for step in range(1, per_section):
         mask_copy(0, step).wait_send()
 
@@ -671,7 +666,7 @@
     def _():
         each_flow(0, lambda copy: copy.wait_send())
 
-    @pl.when(group == SECTIONS - 1)
+    @pl.when(group >= 1)
     def _():
         end_bulk(0)
 

time: 29.3 us -> 28.9 us (0.986)
  Pallas kernels: 28.5 us -> 28.1 us
    pallas_call x1, Pallas kernels: 27.7 us -> 27.3 us  [shards(): pl.pallas_call(functools.partial(chain_kernel, tile_count, grid_cols), ou...]
where the time goes in v5:
time: 28.9 us; the launch traced here: 28.7 us
  Pallas kernels  28.1 us (97%)
  between operations  0.64 us (2%)
    pallas_call x1, Pallas kernels, shards(): pl.pallas_call(functools.partial(chain_kernel, tile_count, grid_cols), ou...  27.3 us
    pallas_call x1, Pallas kernels, shards(): pl.pallas_call(store_kernel, out_shape=(jax.ShapeDtypeStruct(sections.sha...  0.82 us

profile of v5, /device:TPU:0, one launch (start us, length us, event | category | flops | bytes accessed | tf_op | source)
XLA Modules:
  0.0 28.7 jit_solution(6982670215779926290)
XLA Ops:
  0.6 27.3 %chain.1 = (bf16[128,2048]{1,0:T(8,128)(2,1)S(1)}, f32[2,1,16]{2,1,0:T(1,128)S(1)}) custom-call(s32[2,4]{1,0:T(2,128)} %bitcast.1, s32[1,16]{1,0:T(1,128)} %mask_in.1, bf16[256,256]{1,0:T(8,128)(2,1)} %constant.10.clone.left_in, bf16[256,256]{1,0:T(8,128)(2,1)} %constant.11.clone.right_in, f32[2,24,128]{2,1,0:T(8,128)} %constant.12.clone.window_in, ...), custom_call_target="tpu_custom_call" | custom-call | tf_op jit(solution)/shard_map/chain/pallas_call | solution.py:708
  27.9 0.8 %store.1 = (bf16[128,2048]{1,0:T(8,128)(2,1)}, f32[2,1,16]{2,1,0:T(1,128)}) custom-call(bf16[128,2048]{1,0:T(8,128)(2,1)S(1)} %get-tuple-element.4.aligned, f32[2,1,16]{2,1,0:T(1,128)S(1)} %get-tuple-element.5.shift), custom_call_target="tpu_custom_call" | custom-call | tf_op jit(solution)/shard_map/store/pallas_call | solution.py:757

commit v6 on v5

--- a/solution.py
+++ b/solution.py
@@ -17,8 +17,9 @@
 PADDED = 16
 LANES = 128
 CHUNK = 2
+SPAN = 24
 HUB = 2
-REST = 2500
+REST = 1700
 PIECES = 2
 
 sharpness = 12.0
@@ -54,7 +55,7 @@
     left = np.concatenate(left, axis=0)
     right = np.block([[cosine, -sine], [-sine, -cosine]])
     right = np.asarray(right, bf16)
-    u = np.arange(-HALF - REACH, -HALF - REACH + 24)
+    u = np.arange(-HALF - REACH, -HALF - REACH + SPAN)
     window_angle = 2 * np.pi * ((u[:, None] * k[None, :]) % n) / n
     window = np.stack([np.cos(window_angle), np.sin(window_angle)])
     window = window.astype(np.float32)
@@ -63,7 +64,8 @@
     warp = np.zeros((8, n), np.float32)
     warp[:4] = np.stack([np.sin(half_angle), np.cos(half_angle), sign, k])
     parity = (sign[:, None] * sign[None, :]).astype(np.float32)
-    return left, right, window, warp, parity
+    tables = np.concatenate([window[0], window[1], warp, parity], axis=0)
+    return np.stack([left, right]), tables
 
 
 def turn(value):
@@ -139,25 +141,18 @@
     grid_cols,
     offsets_in,
     mask_in,
-    left_in,
-    right_in,
-    window_in,
-    warp_in,
-    parity_in,
+    dft_in,
+    tables_in,
     strip,
     out,
     node_ref,
-    left_ref,
-    right_ref,
-    window,
-    warp_tables,
-    parity_ref,
+    dft_ref,
+    tables,
     whole,
     check,
     offsets,
     mask_ref,
     load_sem,
-    own_raw,
     prev_raw,
     next_raw,
     own_re,
@@ -188,7 +183,7 @@
     rotated = lax.rem(me + tile_count - lead, tile_count)
     group = rotated // per_section
     row = lax.rem(rotated, per_section)
-    chunks, width = own_raw.shape[0], own_raw.shape[2]
+    chunks, width = prev_raw.shape[0], prev_raw.shape[2]
     pair = width // PATCH
     nodes = chunks * pair
     half = lax.rem(group, 2)
@@ -228,14 +223,14 @@
         start = pl.multiple_of((side * chunks + chunk) * width, LANES)
         return strip.at[:, pl.ds(start, width)]
 
+    def strip_half(side):
+        return strip.at[:, pl.ds(pl.multiple_of(side * piece, LANES), piece)]
+
     loads = [
         pltpu.make_async_copy(source, target, load_sem.at[i])
         for i, (source, target) in enumerate(
-            [(mask_in, mask_ref), (offsets_in, offsets), (window_in, window)]
-            + [(left_in, left_ref), (right_in, right_ref)]
-            + [(warp_in, warp_tables), (parity_in, parity_ref)]
-            + [(columns(half, q), own_raw.at[q]) for q in range(chunks)]
-            + [(strip.at[:, pl.ds(k * piece, piece)], whole.at[k]) for k in range(PIECES)]
+            [(mask_in, mask_ref), (offsets_in, offsets), (dft_in, dft_ref), (tables_in, tables)]
+            + [(strip_half(side), whole.at[side]) for side in (half, 1 - half)]
         )
     ]
     for copy in loads:
@@ -247,7 +242,7 @@
         return pltpu.make_async_remote_copy(
             src_ref=columns(1 - half, chunk),
             dst_ref=(prev_raw if way else next_raw).at[chunk],
-            send_sem=bulk_send.at[way, chunk],
+            send_sem=bulk_send.at[way],
             recv_sem=bulk_recv.at[1 - way, chunk],
             device_id={"tile": peer},
             device_id_type=MESH,
@@ -266,8 +261,8 @@
             pltpu.make_async_remote_copy(
                 src_ref=columns(1 - half, k),
                 dst_ref=relay_raw.at[k],
-                send_sem=bulk_send.at[way, k],
-                recv_sem=relay_recv.at[k],
+                send_sem=bulk_send.at[way],
+                recv_sem=relay_recv,
                 device_id={"tile": device(SECTIONS - 1 if way else 0, row - apart)},
                 device_id_type=MESH,
             ).start()
@@ -276,22 +271,20 @@
         return pltpu.make_async_remote_copy(
             src_ref=relay_raw.at[k],
             dst_ref=(prev_raw if way else next_raw).at[k],
-            send_sem=relay_send.at[k],
+            send_sem=relay_send,
             recv_sem=bulk_recv.at[1 - way, k],
             device_id={"tile": device(SECTIONS - 1 if way else 2, row + apart)},
             device_id_type=MESH,
         )
 
-    def forward(way, k):
-        pltpu.make_async_copy(relay_raw.at[k], relay_raw.at[k], relay_recv.at[k]).wait()
-        onward(way, k).start()
+    def forward(way):
+        arrival = relay_raw.at[pl.ds(0, relayed[way])]
+        pltpu.make_async_copy(arrival, arrival, relay_recv).wait()
+        for k in range(relayed[way]):
+            onward(way, k).start()
 
     def release():
         signal(go_sem, SECTIONS - 1, row)
-
-    def end_bulk(way):
-        for chunk in range(chunks):
-            bulk(way, chunk).wait_send()
 
     @pl.when(group == HUB)
     def _():
@@ -317,8 +310,8 @@
         return pltpu.make_async_remote_copy(
             src_ref=mask_tile,
             dst_ref=mask_slots.at[1 - ahead, row],
-            send_sem=mask_send.at[ahead, step],
-            recv_sem=mask_recv.at[1 - ahead, row],
+            send_sem=mask_send.at[ahead],
+            recv_sem=mask_recv.at[1 - ahead],
             device_id={"tile": device(group + ahead, mate(step))},
             device_id_type=MESH,
         )
@@ -328,20 +321,18 @@
     sub = lax.broadcasted_iota(jnp.int32, shape, 0)
     lane = lax.broadcasted_iota(jnp.int32, shape, 1)
     sub_row = lax.rem(sub, per_section)
-    mask_tile[...] = jnp.zeros(shape, f32)
-    mask_tile[0:1, 0:grid_cols] = mask_ref[...].astype(f32)
-    mask_row = mask_tile[0:1, :]
-    mask_tile[...] = jnp.where(sub_row == row, mask_row, 0.0)
+    mask_tile[...] = jnp.zeros((1, LANES), f32)
+    mask_tile[:, 0:grid_cols] = mask_ref[...].astype(f32)
     mask_slots[1, row] = mask_tile[...]
     shift_ref[...] = jnp.zeros((2,) + shape, f32)
 
-    for copy in loads[1:-PIECES]:
+    for copy in loads[1:-1]:
         copy.wait()
 
     eight = lax.broadcasted_iota(jnp.int32, (8, LANES), 0)
 
     def spectra(pixels, kind, first_node):
-        table = left_ref[...]
+        table = dft_ref[0]
         first = mm(table, jnp.concatenate([pixels, pixels], axis=0))
         found = []
         for i in range(pair):
@@ -350,7 +341,7 @@
             top = jnp.where(eight == 0, first[0:8, s] - level, first[0:8, s])
             body = jnp.concatenate([top, first[8:PATCH, s]], axis=0)
             halves = jnp.concatenate([body, first[PATCH:, s]], axis=1).astype(bf16)
-            both = mm(halves, right_ref[...])
+            both = mm(halves, dft_ref[1])
             real, imag = both[:, :PATCH], both[:, PATCH:]
             energy = real * real + imag * imag
             middle = slice(PATCH // 2, PATCH // 2 + 1)
@@ -367,7 +358,7 @@
         return jnp.concatenate([real, imag], axis=1).astype(bf16)
 
     for q in range(chunks):
-        for i, (real, imag) in enumerate(spectra(own_raw[q], 0, q * pair)):
+        for i, (real, imag) in enumerate(spectra(whole[half, :, q * width : (q + 1) * width], 0, q * pair)):
             own_re[q * pair + i] = real
             own_im[q * pair + i] = imag
 
@@ -375,10 +366,9 @@
         k, j = divmod(i, piece // PATCH)
         return whole[k, :, j * PATCH : (j + 1) * PATCH]
 
-    for copy in loads[-PIECES:]:
-        copy.wait()
+    loads[-1].wait()
     for i in range(patches):
-        check[i : i + 1] = jnp.sum(part(i).astype(f32) * parity_ref[...], axis=0, keepdims=True)
+        check[i : i + 1] = jnp.sum(part(i).astype(f32) * tables[2 * SPAN + 8 :], axis=0, keepdims=True)
     sums = jnp.sum(check[...], axis=1, keepdims=True)
     check[...] = jnp.broadcast_to(sums, check.shape)
 
@@ -475,10 +465,10 @@
         variance_b = jnp.maximum((total_b - lost) * size, 0.0) + 1e-05
         scales = (sharpness * size) * lax.rsqrt(variance_a * variance_b)
         corners = end_sy * end_sx * tip_a * tip_b
-        row_cos = window[0, pl.ds(row_offset + REACH, PADDED), :]
-        row_sin = window[1, pl.ds(row_offset + REACH, PADDED), :]
-        col_cos = window[0, pl.ds(col_offset + REACH, PADDED), :]
-        col_sin = window[1, pl.ds(col_offset + REACH, PADDED), :]
+        row_cos = tables[pl.ds(row_offset + REACH, PADDED), :]
+        row_sin = tables[pl.ds(row_offset + REACH + SPAN, PADDED), :]
+        col_cos = tables[pl.ds(col_offset + REACH, PADDED), :]
+        col_sin = tables[pl.ds(col_offset + REACH + SPAN, PADDED), :]
         col_high, col_low = split(jnp.concatenate([col_cos, -col_sin], axis=1))
         moved = []
         for i in range(nodes):
@@ -520,49 +510,56 @@
         flow_col = jnp.sum(plain * across.astype(f32), axis=1, keepdims=True) * inverse
         line_row = jnp.sum(jnp.where(diagonal, flow_row, 0.0), axis=0, keepdims=True)
         line_col = jnp.sum(jnp.where(diagonal, flow_col, 0.0), axis=0, keepdims=True)
-        tile = jnp.where(sub == row, line_row, 0.0)
-        return jnp.where(sub == row + per_section, line_col, tile)
+        return line_row, line_col
 
     def flow_copy(phase, ahead, step):
         part = 1 - phase
         slot = 1 - ahead
         return pltpu.make_async_remote_copy(
             src_ref=flow_tile.at[phase],
-            dst_ref=flow_slots.at[slot, part, row],
-            send_sem=flow_send.at[phase, ahead, step],
-            recv_sem=flow_recv.at[slot, part, row],
+            dst_ref=flow_slots.at[slot, part * per_section + row],
+            send_sem=flow_send.at[phase, ahead],
+            recv_sem=flow_recv.at[slot],
             device_id={"tile": device(group + phase + ahead, mate(step))},
             device_id_type=MESH,
         )
 
-    def each_flow(phase, act):
+    def send_flow(phase, tile):
+        for which in range(2):
+            flow_tile[phase, which : which + 1] = tile[which]
+            if phase == 0:
+                flow_slots[1, per_section + row, which : which + 1] = tile[which]
         for step in range(1 - phase, per_section):
-            act(flow_copy(phase, 0, step))
+            flow_copy(phase, 0, step).start()
 
         @pl.when(group + phase + 1 < SECTIONS)
         def _():
             for step in range(per_section):
-                act(flow_copy(phase, 1, step))
-
-    def take(slots, sems, *where):
-        buffer = slots.at[where]
-        pltpu.make_async_copy(buffer, buffer, sems.at[where]).wait()
+                flow_copy(phase, 1, step).start()
+
+    def drain(ref, sem):
+        pltpu.make_async_copy(ref, ref, sem).wait()
+
+    def end_flow(phase):
+        drain(flow_slots.at[0, pl.ds(0, per_section - 1 + phase)], flow_send.at[phase, 0])
+
+        @pl.when(group + phase + 1 < SECTIONS)
+        def _():
+            drain(flow_slots.at[0, pl.ds(0, per_section)], flow_send.at[phase, 1])
 
     def masks(slot):
-        for step in range(slot, per_section):
-            take(mask_slots, mask_recv, slot, mate(step))
+        drain(mask_slots.at[slot, pl.ds(0, per_section - slot)], mask_recv.at[slot])
 
     def gathered(slot):
         masks(slot)
+        drain(flow_slots.at[slot, pl.ds(0, 2 * per_section - slot)], flow_recv.at[slot])
         flow = jnp.zeros(shape, f32)
         mask = jnp.zeros(shape, f32)
-        for part in range(2):
-            for step in range(1 if slot == 1 and part == 1 else 0, per_section):
-                take(flow_slots, flow_recv, slot, part, mate(step))
-            for line in range(per_section):
-                flow = flow + flow_slots[slot, part, line]
         for line in range(per_section):
-            mask = mask + mask_slots[slot, line]
+            both = flow_slots[slot, line] + flow_slots[slot, per_section + line]
+            flow = jnp.where(sub == line, both[0:1], flow)
+            flow = jnp.where(sub == line + per_section, both[1:2], flow)
+            mask = jnp.where(sub_row == line, mask_slots[slot, line], mask)
         return relax(flow, mask)
 
     @pl.when(group == SECTIONS - 1)
@@ -587,18 +584,14 @@
 
         @pl.when(jnp.logical_and(group == SECTIONS - 1, jnp.logical_not(wrapped)))
         def _():
-            for k in range(relayed[1]):
-                forward(1, k)
+            forward(1)
 
 
         @pl.when(group >= 2)
         def _():
             shift_ref[0] = gathered(0)
 
-        tile = flows(group, down_cross, 0, 1, shift_ref[0])
-        flow_tile[0] = tile
-        flow_slots[1, 1, row] = tile
-        each_flow(0, lambda copy: copy.start())
+        send_flow(0, flows(group, down_cross, 0, 1, shift_ref[0]))
 
     @pl.when(group < SECTIONS - 1)
     def _():
@@ -613,14 +606,12 @@
 
     @pl.when(group < SECTIONS - 1)
     def _():
-        flow_tile[1] = flows(group + 1, up_cross, 2, 0, shift_ref[1])
-        each_flow(1, lambda copy: copy.start())
+        send_flow(1, flows(group + 1, up_cross, 2, 0, shift_ref[1]))
 
         @pl.when(jnp.logical_and(group == 0, jnp.logical_not(wrapped)))
         def _():
             pl.delay(REST)
-            for k in range(relayed[0]):
-                forward(0, k)
+            forward(0)
 
         @pl.when(jnp.logical_and(group == 0, wrapped))
         def _():
@@ -633,14 +624,14 @@
     ]
     for which in range(2):
         node_ref[which] = lines[which][:, :grid_cols]
-    rows = kernel_rows(term_rows(lines[0], lines[1]), warp_tables[...], patches)
+    rows = kernel_rows(term_rows(lines[0], lines[1]), tables[2 * SPAN : 2 * SPAN + 8], patches)
     corner = rows[2] * check[:, 0:1]
     for k in range(PIECES):
         for j in range(piece // PATCH):
             i = k * (piece // PATCH) + j
             moved = warp_patch(part(i), rows[0][i : i + 1], rows[1][i : i + 1])
             out[:, i * PATCH : (i + 1) * PATCH] = (
-                moved - corner[i : i + 1] * parity_ref[...]
+                moved - corner[i : i + 1] * tables[2 * SPAN + 8 :]
             ).astype(bf16)
 
     @pl.when(group == 0)
@@ -651,31 +642,24 @@
     def _():
         masks(0)
 
-    for step in range(1, per_section):
-        mask_copy(0, step).wait_send()
+    drain(mask_slots.at[1, pl.ds(0, per_section - 1)], mask_send.at[0])
 
     @pl.when(group < SECTIONS - 1)
     def _():
-        for step in range(per_section):
-            mask_copy(1, step).wait_send()
-
-        end_bulk(1)
-        each_flow(1, lambda copy: copy.wait_send())
+        drain(mask_slots.at[1, pl.ds(0, per_section)], mask_send.at[1])
+        drain(next_raw, bulk_send.at[1])
+        end_flow(1)
 
     @pl.when(group >= 1)
     def _():
-        each_flow(0, lambda copy: copy.wait_send())
-
-    @pl.when(group >= 1)
-    def _():
-        end_bulk(0)
+        drain(prev_raw, bulk_send.at[0])
+        end_flow(0)
 
     for way, section in ((0, 0), (1, SECTIONS - 1)):
 
         @pl.when(jnp.logical_and(group == section, jnp.logical_not(wrapped)))
         def _():
-            for k in range(relayed[way]):
-                onward(way, k).wait_send()
+            drain(relay_raw.at[pl.ds(0, relayed[way])], relay_send)
 
 
 def store_kernel(aligned, shift, out, shift_out, sems):
@@ -697,7 +681,7 @@
     nodes = chunks * CHUNK
     tile_shape = (2 * per_section, LANES)
     vmem = pl.BlockSpec(memory_space=pltpu.VMEM)
-    left, right, window, warp_tables, parity = constants()
+    dft, tables = constants()
     hbm = pl.BlockSpec(memory_space=pltpu.HBM)
     raw = pltpu.VMEM((chunks, PATCH, width), bf16)
     spectrum = pltpu.VMEM((nodes, PATCH, PATCH), f32)
@@ -711,20 +695,16 @@
             pltpu.VMEM(sections.shape, bf16),
             pltpu.VMEM((2, 1, grid_cols), f32),
         ),
-        in_specs=[hbm] * 8,
+        in_specs=[hbm] * 5,
         out_specs=(vmem, vmem),
         scratch_shapes=[
-            pltpu.VMEM(left.shape, bf16),
-            pltpu.VMEM(right.shape, bf16),
-            pltpu.VMEM(window.shape, f32),
-            pltpu.VMEM(warp_tables.shape, f32),
-            pltpu.VMEM(parity.shape, f32),
+            pltpu.VMEM(dft.shape, bf16),
+            pltpu.VMEM(tables.shape, f32),
             pieces,
             pltpu.VMEM((patches, LANES), f32),
             pltpu.SMEM(coarse_offsets.shape[::-1], jnp.int32),
             pltpu.VMEM(valid_mask.shape, jnp.int32),
-            dma((7 + chunks + PIECES,)),
-            raw,
+            dma((6,)),
             raw,
             raw,
             spectrum,
@@ -732,28 +712,28 @@
             crossed,
             crossed,
             pltpu.VMEM((3, 3, nodes, LANES), f32),
-            pltpu.VMEM(tile_shape, f32),
-            pltpu.VMEM((2, per_section) + tile_shape, f32),
+            pltpu.VMEM((1, LANES), f32),
+            pltpu.VMEM((2, per_section, 1, LANES), f32),
+            pltpu.VMEM((2, 2, LANES), f32),
+            pltpu.VMEM((2, 2 * per_section, 2, LANES), f32),
             pltpu.VMEM((2,) + tile_shape, f32),
-            pltpu.VMEM((2, 2, per_section) + tile_shape, f32),
-            pltpu.VMEM((2,) + tile_shape, f32),
+            dma((2,)),
             dma((2, chunks)),
-            dma((2, chunks)),
-            dma((2, per_section)),
-            dma((2, per_section)),
-            dma((2, 2, per_section)),
-            dma((2, 2, per_section)),
+            dma((2,)),
+            dma((2,)),
+            dma((2, 2)),
+            dma((2,)),
             pltpu.SemaphoreType.REGULAR,
             pltpu.SemaphoreType.REGULAR,
-            raw,
-            dma((chunks,)),
-            dma((chunks,)),
+            pltpu.VMEM((chunks // 2, PATCH, width), bf16),
+            dma(()),
+            dma(()),
         ],
         compiler_params=pltpu.CompilerParams(
             collective_id=0, has_side_effects=True
         ),
         name="chain",
-    )(coarse_offsets.T, valid_mask, left, right, window, warp_tables, parity, sections)
+    )(coarse_offsets.T, valid_mask, dft, tables, sections)
     return pl.pallas_call(
         store_kernel,
         out_shape=(

time: 28.9 us -> 27.8 us (0.962)
  Pallas kernels: 28.1 us -> 27 us
    pallas_call x1, Pallas kernels: 27.3 us -> 26.2 us  [shards(): pl.pallas_call(functools.partial(chain_kernel, tile_count, grid_cols), ou...]
where the time goes in v6:
time: 27.8 us; the launch traced here: 27.6 us
  Pallas kernels  27 us (97%)
  between operations  0.64 us (2%)
    pallas_call x1, Pallas kernels, shards(): pl.pallas_call(functools.partial(chain_kernel, tile_count, grid_cols), ou...  26.2 us
    pallas_call x1, Pallas kernels, shards(): pl.pallas_call(store_kernel, out_shape=(jax.ShapeDtypeStruct(sections.sha...  0.82 us

profile of v6, /device:TPU:0, one launch (start us, length us, event | category | flops | bytes accessed | tf_op | source)
XLA Modules:
  0.0 27.6 jit_solution(13691201415898972884)
XLA Ops:
  0.6 26.2 %chain.1 = (bf16[128,2048]{1,0:T(8,128)(2,1)S(1)}, f32[2,1,16]{2,1,0:T(1,128)S(1)}) custom-call(s32[2,4]{1,0:T(2,128)} %bitcast.1, s32[1,16]{1,0:T(1,128)} %mask_in.1, bf16[2,256,256]{2,1,0:T(8,128)(2,1)} %constant.4.clone.dft_in, f32[184,128]{1,0:T(8,128)} %constant.5.clone.tables_in, bf16[128,2048]{1,0:T(8,128)(2,1)} %strip.1), custom_call_target="tpu_custom_call" | custom-call | tf_op jit(solution)/shard_map/chain/pallas_call | solution.py:692
  26.8 0.8 %store.1 = (bf16[128,2048]{1,0:T(8,128)(2,1)}, f32[2,1,16]{2,1,0:T(1,128)}) custom-call(bf16[128,2048]{1,0:T(8,128)(2,1)S(1)} %get-tuple-element.4.aligned, f32[2,1,16]{2,1,0:T(1,128)S(1)} %get-tuple-element.5.shift), custom_call_target="tpu_custom_call" | custom-call | tf_op jit(solution)/shard_map/store/pallas_call | solution.py:737

commit v7 on v6

--- a/solution.py
+++ b/solution.py
@@ -431,8 +431,7 @@
     corr_row = lax.broadcasted_iota(jnp.int32, (PADDED, PADDED), 0)
     corr_col = lax.broadcasted_iota(jnp.int32, (PADDED, PADDED), 1)
     inside = jnp.logical_and(corr_row < WINDOW, corr_col < WINDOW)
-    gather_sub = lax.broadcasted_iota(jnp.int32, (2 * nodes, nodes * PADDED), 0)
-    gather_lane = lax.broadcasted_iota(jnp.int32, (2 * nodes, nodes * PADDED), 1)
+    eight_lane = lax.broadcasted_iota(jnp.int32, (8, LANES), 1)
     middle = slice(PATCH // 2, PATCH // 2 + 1)
 
     def column(d, which):
@@ -495,21 +494,21 @@
         for i in range(nodes):
             here = correlation[i * PADDED : (i + 1) * PADDED] - corners[i : i + 1] * parity
             weights.append(jnp.where(inside, jnp.exp(here * scales[i : i + 1]), 0.0))
-        high, low = split(jnp.concatenate(weights, axis=0))
-        shifts = (lax.rem(gather_lane, PADDED) - HALF + row_offset).astype(f32)
-        gather = jnp.where(gather_sub < nodes, 1.0, shifts)
-        block = gather_lane // PADDED == lax.rem(gather_sub, nodes)
-        gather = jnp.where(block, gather, 0.0).astype(bf16)
-        sums = mm(
-            jnp.concatenate([gather, gather], axis=1), jnp.concatenate([high, low], axis=0)
-        )
-        plain = sums[:nodes]
-        across = lax.broadcasted_iota(jnp.int32, (nodes, PADDED), 1) - HALF + col_offset
-        inverse = 1.0 / jnp.sum(plain, axis=1, keepdims=True)
-        flow_row = jnp.sum(sums[nodes:], axis=1, keepdims=True) * inverse
-        flow_col = jnp.sum(plain * across.astype(f32), axis=1, keepdims=True) * inverse
-        line_row = jnp.sum(jnp.where(diagonal, flow_row, 0.0), axis=0, keepdims=True)
-        line_col = jnp.sum(jnp.where(diagonal, flow_col, 0.0), axis=0, keepdims=True)
+        across = (lax.broadcasted_iota(jnp.int32, (8, PADDED), 1) - HALF + col_offset).astype(f32)
+        down = (lax.broadcasted_iota(jnp.int32, (8, PADDED), 0) - HALF + row_offset).astype(f32)
+        sums = [jnp.zeros((8, LANES), f32) for _ in range(3)]
+        for i in range(nodes):
+            upper, lower = weights[i][:8], weights[i][8:]
+            plain = upper + lower
+            parts = (plain, upper * down + lower * (down + 8.0), plain * across)
+            here = eight_lane == base + i
+            for k in range(3):
+                line = jnp.sum(parts[k], axis=1, keepdims=True)
+                sums[k] = jnp.where(here, line, sums[k])
+        plain, line_row, line_col = [jnp.sum(value, axis=0, keepdims=True) for value in sums]
+        inverse = 1.0 / jnp.where(plain > 0.0, plain, 1.0)
+        line_row = line_row * inverse
+        line_col = line_col * inverse
         return line_row, line_col
 
     def flow_copy(phase, ahead, step):

time: 27.8 us -> 27.5 us (0.989)
  Pallas kernels: 27 us -> 26.7 us
    pallas_call x1, Pallas kernels: 26.2 us -> 25.9 us  [shards(): pl.pallas_call(functools.partial(chain_kernel, tile_count, grid_cols), ou...]
where the time goes in v7:
time: 27.5 us; the launch traced here: 27.3 us
  Pallas kernels  26.7 us (97%)
  between operations  0.64 us (2%)
    pallas_call x1, Pallas kernels, shards(): pl.pallas_call(functools.partial(chain_kernel, tile_count, grid_cols), ou...  25.9 us
    pallas_call x1, Pallas kernels, shards(): pl.pallas_call(store_kernel, out_shape=(jax.ShapeDtypeStruct(sections.sha...  0.82 us

profile of v7, /device:TPU:0, one launch (start us, length us, event | category | flops | bytes accessed | tf_op | source)
XLA Modules:
  0.0 27.3 jit_solution(12877828326899662281)
XLA Ops:
  0.6 25.9 %chain.1 = (bf16[128,2048]{1,0:T(8,128)(2,1)S(1)}, f32[2,1,16]{2,1,0:T(1,128)S(1)}) custom-call(s32[2,4]{1,0:T(2,128)} %bitcast.1, s32[1,16]{1,0:T(1,128)} %mask_in.1, bf16[2,256,256]{2,1,0:T(8,128)(2,1)} %constant.4.clone.dft_in, f32[184,128]{1,0:T(8,128)} %constant.5.clone.tables_in, bf16[128,2048]{1,0:T(8,128)(2,1)} %strip.1), custom_call_target="tpu_custom_call" | custom-call | tf_op jit(solution)/shard_map/chain/pallas_call | solution.py:691
  26.5 0.8 %store.1 = (bf16[128,2048]{1,0:T(8,128)(2,1)}, f32[2,1,16]{2,1,0:T(1,128)}) custom-call(bf16[128,2048]{1,0:T(8,128)(2,1)S(1)} %get-tuple-element.4.aligned, f32[2,1,16]{2,1,0:T(1,128)S(1)} %get-tuple-element.5.shift), custom_call_target="tpu_custom_call" | custom-call | tf_op jit(solution)/shard_map/store/pallas_call | solution.py:736

commit v8 on v7

--- a/solution.py
+++ b/solution.py
@@ -19,8 +19,10 @@
 CHUNK = 2
 SPAN = 24
 HUB = 2
-REST = 1700
+REST = 1400
+LAG = 500
 PIECES = 2
+ORDER = 1
 
 sharpness = 12.0
 anchor_weight = 2.0
@@ -82,15 +84,19 @@
     whole = jnp.round(d)
     frac = d - whole
     odd = jnp.abs(whole - 2.0 * jnp.round(whole * 0.5))
-    sine = jnp.sin(jnp.pi * frac)
+    wide = frac * np.pi
+    square = wide * wide
+    shape = 1.0 + square * (-1 / 6 + square * (1 / 120 + square * (
+        -1 / 5040 + square * (1 / 362880 - square * (1 / 39916800)))))
+    sine = wide * shape
     signed = jnp.where(odd > 0.5, -sine, sine) * (1.0 / PATCH)
     angle = d * (np.pi / PATCH)
-    tangent = jnp.sin(angle) / jnp.cos(angle)
+    square = angle * angle
+    tangent = angle * (1.0 + square * (1 / 3 + square * (2 / 15 + square * (
+        17 / 315 + square * (62 / 2835 + square * (1382 / 155925))))))
     small = frac * (np.pi / PATCH)
-    tiny = jnp.abs(frac) < 1e-6
-    peak = jnp.where(
-        tiny, 1.0, sine * jnp.cos(small) / jnp.where(tiny, 1.0, PATCH * jnp.sin(small))
-    )
+    square = small * small
+    peak = shape * (1.0 - square * (1 / 3 + square * (1 / 45)))
     return tangent, signed, peak, whole
 
 
@@ -253,6 +259,10 @@
             bulk(way, chunk).start()
 
     relayed = (chunks // 2, chunks // 2)
+    arrival = [
+        sorted(range(chunks), key=lambda q: (q - n if q >= n else q, ORDER * (q < n)))
+        for n in (relayed[1], relayed[0])
+    ]
     apart = per_section - per_section // 2
     wrapped = row >= apart
 
@@ -337,7 +347,8 @@
         found = []
         for i in range(pair):
             s = slice(i * PATCH, (i + 1) * PATCH)
-            level = jnp.sum(first[0:1, s], axis=1, keepdims=True) * (1.0 / PATCH)
+            level = jnp.sum(pixels[:, s].astype(f32), axis=0, keepdims=True)
+            level = jnp.sum(level, axis=1, keepdims=True) * (1.0 / PATCH)
             top = jnp.where(eight == 0, first[0:8, s] - level, first[0:8, s])
             body = jnp.concatenate([top, first[8:PATCH, s]], axis=0)
             halves = jnp.concatenate([body, first[PATCH:, s]], axis=1).astype(bf16)
@@ -346,9 +357,10 @@
             energy = real * real + imag * imag
             middle = slice(PATCH // 2, PATCH // 2 + 1)
             node = first_node + i
-            stats[kind, 0, node : node + 1] = jnp.sum(energy, axis=0, keepdims=True)
-            stats[kind, 1, node : node + 1] = energy[middle]
-            stats[kind, 2, node : node + 1] = real[middle]
+            where = pl.ds(node, 1)
+            stats[kind, 0, where] = jnp.sum(energy, axis=0, keepdims=True)
+            stats[kind, 1, where] = energy[middle]
+            stats[kind, 2, where] = real[middle]
             found.append((real, imag))
         return found
 
@@ -406,21 +418,6 @@
     left_ok = jnp.logical_and(lane > 0, lane < grid_cols).astype(f32)
     right_ok = (lane < grid_cols - 1).astype(f32)
     count = up_ok + down_ok + left_ok + right_ok
-
-    def relax(flow, mask):
-        weight = anchor_weight * mask
-        pull = weight * flow
-        scale = 1.0 / (weight + count)
-        d = flow * mask
-        for _ in range(SWEEPS):
-            near = (
-                up_ok * pltpu.roll(d, 1, 0)
-                + down_ok * pltpu.roll(d, 2 * per_section - 1, 0)
-                + left_ok * pltpu.roll(d, 1, 1)
-                + right_ok * pltpu.roll(d, LANES - 1, 1)
-            )
-            d = (pull + near) * scale
-        return jnp.where(lane < grid_cols, d, 0.0)
 
     node_sub = lax.broadcasted_iota(jnp.int32, (nodes, LANES), 0)
     node_lane = lax.broadcasted_iota(jnp.int32, (nodes, LANES), 1)
@@ -551,15 +548,28 @@
 
     def gathered(slot):
         masks(slot)
+        mask = jnp.zeros(shape, f32)
+        for line in range(per_section):
+            mask = jnp.where(sub_row == line, mask_slots[slot, line], mask)
+        weight = anchor_weight * mask
+        scale = 1.0 / (weight + count)
+        weight = weight * scale
+        up, down = up_ok * scale, down_ok * scale
+        left, right = left_ok * scale, right_ok * scale
         drain(flow_slots.at[slot, pl.ds(0, 2 * per_section - slot)], flow_recv.at[slot])
         flow = jnp.zeros(shape, f32)
-        mask = jnp.zeros(shape, f32)
         for line in range(per_section):
             both = flow_slots[slot, line] + flow_slots[slot, per_section + line]
             flow = jnp.where(sub == line, both[0:1], flow)
             flow = jnp.where(sub == line + per_section, both[1:2], flow)
-            mask = jnp.where(sub_row == line, mask_slots[slot, line], mask)
-        return relax(flow, mask)
+        pull = weight * flow
+        d = flow * mask
+        for _ in range(SWEEPS):
+            d = pull + (
+                (up * pltpu.roll(d, 1, 0) + down * pltpu.roll(d, 2 * per_section - 1, 0))
+                + (left * pltpu.roll(d, 1, 1) + right * pltpu.roll(d, LANES - 1, 1))
+            )
+        return jnp.where(lane < grid_cols, d, 0.0)
 
     @pl.when(group == SECTIONS - 1)
     def _():
@@ -573,9 +583,10 @@
     @pl.when(group >= 1)
     def _():
         for q in range(chunks):
-            arrived(0, q)
-            for i, found in enumerate(spectra(prev_raw[q], 1, q * pair)):
-                down_cross[q * pair + i] = cross(own(q * pair + i), found)
+            c = jnp.where(group == SECTIONS - 1, arrival[0][q], q)
+            arrived(0, c)
+            for i, found in enumerate(spectra(prev_raw[c], 1, c * pair)):
+                down_cross[c * pair + i] = cross(own(c * pair + i), found)
 
         @pl.when(jnp.logical_and(group == 2, wrapped))
         def _():
@@ -595,9 +606,10 @@
     @pl.when(group < SECTIONS - 1)
     def _():
         for q in range(chunks):
-            arrived(1, q)
-            for i, found in enumerate(spectra(next_raw[q], 2, q * pair)):
-                up_cross[q * pair + i] = cross(found, own(q * pair + i))
+            c = jnp.where(group == 2, arrival[1][q], q)
+            arrived(1, c)
+            for i, found in enumerate(spectra(next_raw[c], 2, c * pair)):
+                up_cross[c * pair + i] = cross(found, own(c * pair + i))
 
     @pl.when(group >= 1)
     def _():
@@ -610,6 +622,11 @@
         @pl.when(jnp.logical_and(group == 0, jnp.logical_not(wrapped)))
         def _():
             pl.delay(REST)
+
+            @pl.when(lax.rem(me, 2) == 1)
+            def _():
+                pl.delay(LAG)
+
             forward(0)
 
         @pl.when(jnp.logical_and(group == 0, wrapped))

time: 27.5 us -> 26.9 us (0.978)
  Pallas kernels: 26.7 us -> 26.2 us
    pallas_call x1, Pallas kernels: 25.9 us -> 25.3 us  [shards(): pl.pallas_call(functools.partial(chain_kernel, tile_count, grid_cols), ou...]
where the time goes in v8:
time: 26.9 us; the launch traced here: 26.8 us
  Pallas kernels  26.2 us (97%)
  between operations  0.64 us (2%)
    pallas_call x1, Pallas kernels, shards(): pl.pallas_call(functools.partial(chain_kernel, tile_count, grid_cols), ou...  25.3 us
    pallas_call x1, Pallas kernels, shards(): pl.pallas_call(store_kernel, out_shape=(jax.ShapeDtypeStruct(sections.sha...  0.82 us

profile of v8, /device:TPU:0, one launch (start us, length us, event | category | flops | bytes accessed | tf_op | source)
XLA Modules:
  0.0 26.8 jit_solution(11399692955244901014)
XLA Ops:
  0.6 25.3 %chain.1 = (bf16[128,2048]{1,0:T(8,128)(2,1)S(1)}, f32[2,1,16]{2,1,0:T(1,128)S(1)}) custom-call(s32[2,4]{1,0:T(2,128)} %bitcast.1, s32[1,16]{1,0:T(1,128)} %mask_in.1, bf16[2,256,256]{2,1,0:T(8,128)(2,1)} %constant.4.clone.dft_in, f32[184,128]{1,0:T(8,128)} %constant.5.clone.tables_in, bf16[128,2048]{1,0:T(8,128)(2,1)} %strip.1), custom_call_target="tpu_custom_call" | custom-call | tf_op jit(solution)/shard_map/chain/pallas_call | solution.py:708
  26.0 0.8 %store.1 = (bf16[128,2048]{1,0:T(8,128)(2,1)}, f32[2,1,16]{2,1,0:T(1,128)}) custom-call(bf16[128,2048]{1,0:T(8,128)(2,1)S(1)} %get-tuple-element.4.aligned, f32[2,1,16]{2,1,0:T(1,128)S(1)} %get-tuple-element.5.shift), custom_call_target="tpu_custom_call" | custom-call | tf_op jit(solution)/shard_map/store/pallas_call | solution.py:753

commit v9 on v8

--- a/solution.py
+++ b/solution.py
@@ -344,15 +344,17 @@
     def spectra(pixels, kind, first_node):
         table = dft_ref[0]
         first = mm(table, jnp.concatenate([pixels, pixels], axis=0))
-        found = []
+        found, rows = [], []
         for i in range(pair):
             s = slice(i * PATCH, (i + 1) * PATCH)
             level = jnp.sum(pixels[:, s].astype(f32), axis=0, keepdims=True)
             level = jnp.sum(level, axis=1, keepdims=True) * (1.0 / PATCH)
             top = jnp.where(eight == 0, first[0:8, s] - level, first[0:8, s])
             body = jnp.concatenate([top, first[8:PATCH, s]], axis=0)
-            halves = jnp.concatenate([body, first[PATCH:, s]], axis=1).astype(bf16)
-            both = mm(halves, dft_ref[1])
+            rows.append(jnp.concatenate([body, first[PATCH:, s]], axis=1).astype(bf16))
+        every = mm(jnp.concatenate(rows, axis=0), dft_ref[1])
+        for i in range(pair):
+            both = every[i * PATCH : (i + 1) * PATCH]
             real, imag = both[:, :PATCH], both[:, PATCH:]
             energy = real * real + imag * imag
             middle = slice(PATCH // 2, PATCH // 2 + 1)

time: 26.9 us -> 26.9 us (level)
  no operation moved by 1% of the time
where the time goes in v9:
time: 26.9 us; the launch traced here: 26.8 us
  Pallas kernels  26.2 us (97%)
  between operations  0.64 us (2%)
    pallas_call x1, Pallas kernels, shards(): pl.pallas_call(functools.partial(chain_kernel, tile_count, grid_cols), ou...  25.3 us
    pallas_call x1, Pallas kernels, shards(): pl.pallas_call(store_kernel, out_shape=(jax.ShapeDtypeStruct(sections.sha...  0.82 us

profile of v9, /device:TPU:0, one launch (start us, length us, event | category | flops | bytes accessed | tf_op | source)
XLA Modules:
  0.0 26.8 jit_solution(17012497613668835374)
XLA Ops:
  0.6 25.3 %chain.1 = (bf16[128,2048]{1,0:T(8,128)(2,1)S(1)}, f32[2,1,16]{2,1,0:T(1,128)S(1)}) custom-call(s32[2,4]{1,0:T(2,128)} %bitcast.1, s32[1,16]{1,0:T(1,128)} %mask_in.1, bf16[2,256,256]{2,1,0:T(8,128)(2,1)} %constant.4.clone.dft_in, f32[184,128]{1,0:T(8,128)} %constant.5.clone.tables_in, bf16[128,2048]{1,0:T(8,128)(2,1)} %strip.1), custom_call_target="tpu_custom_call" | custom-call | tf_op jit(solution)/shard_map/chain/pallas_call | solution.py:710
  26.0 0.8 %store.1 = (bf16[128,2048]{1,0:T(8,128)(2,1)}, f32[2,1,16]{2,1,0:T(1,128)}) custom-call(bf16[128,2048]{1,0:T(8,128)(2,1)S(1)} %get-tuple-element.4.aligned, f32[2,1,16]{2,1,0:T(1,128)S(1)} %get-tuple-element.5.shift), custom_call_target="tpu_custom_call" | custom-call | tf_op jit(solution)/shard_map/store/pallas_call | solution.py:755

commit v10 on v9

--- a/solution.py
+++ b/solution.py
@@ -516,7 +516,7 @@
         return pltpu.make_async_remote_copy(
             src_ref=flow_tile.at[phase],
             dst_ref=flow_slots.at[slot, part * per_section + row],
-            send_sem=flow_send.at[phase, ahead],
+            send_sem=flow_send.at[phase],
             recv_sem=flow_recv.at[slot],
             device_id={"tile": device(group + phase + ahead, mate(step))},
             device_id_type=MESH,
@@ -539,11 +539,15 @@
         pltpu.make_async_copy(ref, ref, sem).wait()
 
     def end_flow(phase):
-        drain(flow_slots.at[0, pl.ds(0, per_section - 1 + phase)], flow_send.at[phase, 0])
+        near = per_section - 1 + phase
 
         @pl.when(group + phase + 1 < SECTIONS)
         def _():
-            drain(flow_slots.at[0, pl.ds(0, per_section)], flow_send.at[phase, 1])
+            drain(flow_slots.at[0, pl.ds(0, near + per_section)], flow_send.at[phase])
+
+        @pl.when(group + phase + 1 >= SECTIONS)
+        def _():
+            drain(flow_slots.at[0, pl.ds(0, near)], flow_send.at[phase])
 
     def masks(slot):
         drain(mask_slots.at[slot, pl.ds(0, per_section - slot)], mask_recv.at[slot])
@@ -739,7 +743,7 @@
             dma((2, chunks)),
             dma((2,)),
             dma((2,)),
-            dma((2, 2)),
+            dma((2,)),
             dma((2,)),
             pltpu.SemaphoreType.REGULAR,
             pltpu.SemaphoreType.REGULAR,

time: 26.9 us -> 26.9 us (level)
  no operation moved by 1% of the time
where the time goes in v10:
time: 26.9 us; the launch traced here: 26.8 us
  Pallas kernels  26.1 us (97%)
  between operations  0.64 us (2%)
    pallas_call x1, Pallas kernels, shards(): pl.pallas_call(functools.partial(chain_kernel, tile_count, grid_cols), ou...  25.3 us
    pallas_call x1, Pallas kernels, shards(): pl.pallas_call(store_kernel, out_shape=(jax.ShapeDtypeStruct(sections.sha...  0.82 us

profile of v10, /device:TPU:0, one launch (start us, length us, event | category | flops | bytes accessed | tf_op | source)
XLA Modules:
  0.0 26.8 jit_solution(12955303757427602367)
XLA Ops:
  0.6 25.3 %chain.1 = (bf16[128,2048]{1,0:T(8,128)(2,1)S(1)}, f32[2,1,16]{2,1,0:T(1,128)S(1)}) custom-call(s32[2,4]{1,0:T(2,128)} %bitcast.1, s32[1,16]{1,0:T(1,128)} %mask_in.1, bf16[2,256,256]{2,1,0:T(8,128)(2,1)} %constant.4.clone.dft_in, f32[184,128]{1,0:T(8,128)} %constant.5.clone.tables_in, bf16[128,2048]{1,0:T(8,128)(2,1)} %strip.1), custom_call_target="tpu_custom_call" | custom-call | tf_op jit(solution)/shard_map/chain/pallas_call | solution.py:714
  26.0 0.8 %store.1 = (bf16[128,2048]{1,0:T(8,128)(2,1)}, f32[2,1,16]{2,1,0:T(1,128)}) custom-call(bf16[128,2048]{1,0:T(8,128)(2,1)S(1)} %get-tuple-element.4.aligned, f32[2,1,16]{2,1,0:T(1,128)S(1)} %get-tuple-element.5.shift), custom_call_target="tpu_custom_call" | custom-call | tf_op jit(solution)/shard_map/store/pallas_call | solution.py:759
